TPU v7x, 256 devices: a whole 4x4x8 slice. The times are simulated.
256 devices in a mesh: tm: 32 (over z, x), rows: 8 (over y, core).
Axes of the slice: x: 4, y: 4, z: 8, core: 2. Of those that a mesh axis runs over, the one named last changes fastest.
Arguments:
- x_start: float32 [1, 16, 128, 128], P(None, None, 'rows'), may hold values from -6 to 6
- noise: float32 [32, 1, 16, 128, 128], P('tm', None, None, 'rows'), may hold values from -6 to 6
- fresh: float32 [5, 1, 16, 128, 128], P(None, None, None, 'rows'), may hold values from -6 to 6
- sched: int32 [38], replicated, may hold values from 888 to 999, as said below
- conv_in: bfloat16 [3, 3, 192, 16], replicated, may hold values from -0.5 to 0.5
- conv_mid: bfloat16 [3, 3, 192, 192], replicated, may hold values from -0.15625 to 0.15625
- conv_out: bfloat16 [3, 3, 16, 192], replicated, may hold values from -0.15625 to 0.15625
- time_weight: bfloat16 [192, 192], replicated, may hold values from -0.4375 to 0.4375
Outputs:
- trajectory: float32 [2, 32, 1, 16, 128, 128], P(None, 'tm', None, None, 'rows')
Inputs may be any that keep to these rules, and one draw needn't show every extreme that they name: sched[0] = 999 and each entry is 1 to 3 below the one before it.
All inputs are finite; a program needn't handle non-finite values.
Results may differ from a plain program's by a relative error of at most 0.00055.
Values may be sent and summed in bfloat16 or wider, within the bound.
No kernel may reach another device: no remote copies, remote signals or barrier semaphores. Data moves between devices by JAX's collectives and lax.ppermute only.
A program may use at most 64 MiB of HBM per device.

v0:
```python
import jax
import jax.numpy as jnp
from jax import lax
from jax.sharding import PartitionSpec as P

STEPS = 1000
SWEEPS = 2
RETIRE = 5
ROUNDS = 2


log_base = 9.210340371976184


def extended(array, sides, width):
    for axis, dim in sides:
        size, length = (lax.axis_size(axis), array.shape[dim])
        up = [(i, (i + 1) % size) for i in range(size - 1)]
        down = [(j, i) for i, j in up]
        last = lax.slice_in_dim(array, length - width, length, axis=dim)
        initial = lax.slice_in_dim(array, 0, width, axis=dim)
        before = lax.ppermute(last, axis, up)
        after = lax.ppermute(initial, axis, down)
        array = jnp.concatenate([before, array, after], axis=dim)
    return array


def entering_2(value, axis, join, neutral):
    count, mine = (lax.axis_size(axis), lax.axis_index(axis))
    pieces = lax.all_gather(value, axis)
    subtotal = jnp.full_like(value, 0) + jnp.asarray(neutral, value.dtype)

    def turn(position, subtotal):
        longer = join(subtotal, pieces[position])
        return jnp.where(position < mine, longer, subtotal)

    return lax.fori_loop(0, count - 1, turn, subtotal)


def from_behind(array, axis, by):
    length = lax.axis_size(axis)
    pairs = [(i, i + by) for i in range(length) if 0 <= i + by < length]
    return lax.ppermute(array, axis, pairs)


def broadcast(value, axis, source):
    kept = jnp.where(lax.axis_index(axis) == source, value, 0).astype(value.dtype)
    return lax.psum(kept, axis)


def plan_table(total_steps):
    positions = jnp.arange(total_steps).astype(jnp.float32)
    betas = 0.0001 + (0.02 - 0.0001) * positions / (total_steps - 1)
    return jnp.cumsum(jnp.log(1.0 - betas))


def lookup(table, position):
    return jnp.sum(jnp.where(jnp.arange(table.shape[0]) == position, table, 0.0))


def coefficients(log_now, log_next):
    retained = jnp.exp(log_now - log_next)
    bar_now = jnp.exp(log_now)
    bar_next = jnp.exp(log_next)
    keep = 1.0 / jnp.sqrt(retained) - 1.0
    predict = -(1.0 - retained) / (jnp.sqrt(1.0 - bar_now) * jnp.sqrt(retained))
    spread = jnp.sqrt((1.0 - bar_next) / (1.0 - bar_now) * (1.0 - retained))
    return (keep, predict, spread)


def time_features(now_value, width):
    half = width // 2
    freqs = jnp.exp(-log_base * jnp.arange(half).astype(jnp.float32) / half)
    angles = now_value * freqs
    return jnp.concatenate([jnp.sin(angles), jnp.cos(angles)], axis=-1)


def convolve(padded, weight, out_rows):
    columns = padded.shape[3]
    widened = jnp.pad(padded, ((0, 0), (0, 0), (0, 0), (1, 1)))
    running = None
    for row_tap in range(3):
        for col_tap in range(3):
            shifted = widened[:, :, row_tap : row_tap + out_rows, col_tap : col_tap + columns]
            product_term = jnp.einsum(
                "oc,fcrw->forw",
                weight[row_tap, col_tap],
                shifted,
                preferred_element_type=jnp.float32,
            )
            running = product_term if running is None else running + product_term
    return running


def hidden_rim(values):
    return extended(values, (("rows", 2),), 1)


def drift_network(state, noise_now, keep, predict, spread, embedding, conv_in, conv_mid, conv_out):
    latent = state[0].astype(jnp.bfloat16)
    strip_rows = latent.shape[2]
    padded = extended(latent, (("rows", 2),), 1)
    first = convolve(padded, conv_in, strip_rows) + embedding[None, :, None, None]
    first = jax.nn.silu(first).astype(jnp.bfloat16)
    second = jax.nn.silu(convolve(hidden_rim(first), conv_mid, strip_rows)).astype(jnp.bfloat16)
    predicted = convolve(hidden_rim(second), conv_out, strip_rows)
    return keep * state + predict * predicted[None] + spread * noise_now


def add_terms(earlier, later):
    return earlier + later


def prefix(change):
    return entering_2(change, "tm", add_terms, jnp.zeros_like(change))


def shards(x_start, noise, fresh, sched, conv_in, conv_mid, conv_out, time_weight):
    slot = lax.axis_index("tm")
    slots = lax.axis_size("tm")
    table = plan_table(STEPS)
    hidden_width = conv_mid.shape[2]
    state = x_start[None]
    noise_now = noise
    base_state = state
    snapshots = []
    for round_index in range(ROUNDS):
        position = slot + RETIRE * round_index
        now_step = lax.dynamic_index_in_dim(sched, position, 0, keepdims=False)
        next_step = lax.dynamic_index_in_dim(sched, position + 1, 0, keepdims=False)
        keep, predict, spread = coefficients(lookup(table, now_step), lookup(table, next_step))
        features = time_features(now_step.astype(jnp.float32), hidden_width)
        embedding = jnp.dot(
            features[None], time_weight.astype(jnp.float32), precision=lax.Precision.HIGHEST
        )[0]
        for sweep_index in range(SWEEPS):
            change = drift_network(
                state, noise_now, keep, predict, spread, embedding, conv_in, conv_mid, conv_out
            )
            state = base_state + prefix(change)
        snapshots.append(state)
        if round_index + 1 < ROUNDS:
            moved_state, moved_noise = from_behind((state, noise_now), "tm", -RETIRE)
            entering = slot >= slots - RETIRE
            pick = jnp.clip(round_index * RETIRE + slot - (slots - RETIRE), 0, fresh.shape[0] - 1)
            incoming = lax.dynamic_index_in_dim(fresh, pick, 0, keepdims=True)
            state = jnp.where(entering, state, moved_state)
            noise_now = jnp.where(entering, incoming, moved_noise)
            base_state = broadcast(state, "tm", 0)
    return jnp.stack(snapshots)


def solution(mesh):
    placed = (
        P(None, None, "rows", None),
        P("tm", None, None, "rows", None),
        P(None, None, None, "rows", None),
        P(),
        P(),
        P(),
        P(),
        P(),
    )
    return jax.shard_map(
        shards,
        mesh=mesh,
        in_specs=placed,
        out_specs=P(None, "tm", None, None, "rows", None),
        check_vma=False,
    )
```

profile of v0, /device:TPU:1, one launch (start us, length us, event | category | flops | bytes accessed | tf_op | source)
XLA Modules:
  0.0 732.4 jit_solution(4137733619743370829)
XLA Ops:
  6.5 1.0 copy.87
  7.6 4.6 collective-permute-start
  12.2 1.9 collective-permute-start.1
  14.1 1.5 fusion.526
  16.3 1.1 fusion.299
  18.1 3.2 select_reduce_fusion
  27.1 1.2 fusion.34
  28.3 3.6 collective-permute-start.2
  32.0 1.9 collective-permute-start.3
  34.3 3.1 collective-permute-done.3
  41.1 1.2 fusion.30
  42.3 1.9 collective-permute-start.4
  44.3 2.6 collective-permute-start.5
  47.1 2.6 collective-permute-done.5
  54.3 80.5 %all-gather.9.cloned.1.call-done = f32[32,1,16,16,128]{4,3,2,1,0:T(8,128)} async-done(((f32[1,1,16,16,128]{4,3,2,1,0:T(8,128)}), f32[32,1,16,16,128]{4,3,2,1,0:T(8,128)}) %all-gather.9.cloned.1.call-update) | async-done | bytes 4194320 | tf_op jit(solution)/shard_map/all_gather | solution.py:30
  134.7 30.1 %while.56 = (s32[]{:T(128)}, f32[1,1,16,16,128]{4,3,2,1,0:T(8,128)S(1)}, s32[]{:T(128)}, f32[32,1,1,16,16,128]{5,4,3,2,1,0:T(8,128)}, s32[]{:T(128)}, /*index=5*/s32[]{:T(128)}) while((s32[]{:T(128)}, f32[1,1,16,16,128]{4,3,2,1,0:T(8,128)S(1)}, s32[]{:T(128)}, f32[32,1,1,16,16,128]{5,4,3,2,1,0:T(8,128)}, s32[]{:T(128)}, ...), condition=%wide.region_5.6_spmd.clone, body=%wide.region_4.5_spmd.clone.sunk | while | flops 98308 | bytes 393309 | solution.py:37
  165.0 7.2 collective-permute-start.6
  172.2 1.9 collective-permute-start.7
  174.5 2.6 collective-permute-done.7
  180.1 1.1 fusion.35
  181.3 2.0 collective-permute-start.8
  183.2 2.4 collective-permute-start.9
  186.0 2.7 collective-permute-done.9
  192.4 1.2 fusion.31
  193.6 1.9 collective-permute-start.10
  195.5 2.6 collective-permute-start.11
  198.3 2.6 collective-permute-done.11
  205.0 1.3 collective-permute-start.19
  207.0 72.3 %all-gather.11.cloned.1.call-done = f32[32,1,16,16,128]{4,3,2,1,0:T(8,128)} async-done(((f32[1,1,16,16,128]{4,3,2,1,0:T(8,128)}), f32[32,1,16,16,128]{4,3,2,1,0:T(8,128)}) %all-gather.11.cloned.1.call-update) | async-done | bytes 4194320 | tf_op jit(solution)/shard_map/all_gather | solution.py:30
  279.3 30.1 %while.57 = (s32[]{:T(128)}, f32[1,1,16,16,128]{4,3,2,1,0:T(8,128)S(1)}, s32[]{:T(128)}, f32[32,1,1,16,16,128]{5,4,3,2,1,0:T(8,128)}, s32[]{:T(128)}, /*index=5*/s32[]{:T(128)}) while((s32[]{:T(128)}, f32[1,1,16,16,128]{4,3,2,1,0:T(8,128)S(1)}, s32[]{:T(128)}, f32[32,1,1,16,16,128]{5,4,3,2,1,0:T(8,128)}, s32[]{:T(128)}, ...), condition=%wide.region_7.8_spmd.clone, body=%wide.region_6.7_spmd.clone.sunk | while | flops 98308 | bytes 393309 | solution.py:37
  309.5 1.3 collective-permute-start.12
  313.9 2.3 collective-permute-done.12
  316.1 8.4 %collective-permute-start.13 = (bf16[1,16,1,128]{3,1,2,0:T(8,128)(2,1)S(1)}, bf16[1,16,1,128]{3,1,2,0:T(8,128)(2,1)S(1)}, u32[]{:S(2)}, u32[]{:S(2)}) collective-permute-start(bf16[1,16,1,128]{3,1,2,0:T(8,128)(2,1)S(1)} %get-tuple-element.489), channel_id=1, source_target_pairs={{0,1},{1,2},{2,3},{3,4},{4,5},{5,6},{6,7},{8,9},{9,10},{10,11},{11... | collective-permute-start | bytes 12296 | tf_op jit(solution)/shard_map/ppermute | solution.py:22
  324.5 1.9 collective-permute-start.14
  326.9 2.6 collective-permute-done.14
  332.5 1.1 fusion.36
  333.6 2.0 collective-permute-start.15
  335.6 2.4 collective-permute-start.16
  338.3 2.7 collective-permute-done.16
  344.7 1.2 fusion.32
  345.9 1.9 collective-permute-start.17
  347.8 2.8 collective-permute-start.18
  350.9 2.4 collective-permute-done.18
  358.1 76.6 %all-gather.13.cloned.1.call-done = f32[32,1,16,16,128]{4,3,2,1,0:T(8,128)} async-done(((f32[1,1,16,16,128]{4,3,2,1,0:T(8,128)}), f32[32,1,16,16,128]{4,3,2,1,0:T(8,128)}) %all-gather.13.cloned.1.call-update) | async-done | bytes 4194320 | tf_op jit(solution)/shard_map/all_gather | solution.py:30
  434.7 30.1 %while.58 = (s32[]{:T(128)}, f32[1,1,16,16,128]{4,3,2,1,0:T(8,128)S(1)}, s32[]{:T(128)}, f32[32,1,1,16,16,128]{5,4,3,2,1,0:T(8,128)}, s32[]{:T(128)}, /*index=5*/s32[]{:T(128)}) while((s32[]{:T(128)}, f32[1,1,16,16,128]{4,3,2,1,0:T(8,128)S(1)}, s32[]{:T(128)}, f32[32,1,1,16,16,128]{5,4,3,2,1,0:T(8,128)}, s32[]{:T(128)}, ...), condition=%wide.region_12.13_spmd.clone, body=%wide.region_11.12_spmd.clone.sunk | while | flops 98308 | bytes 393309 | solution.py:37
  448.3 1.0 add_select_fusion.10
  457.1 1.0 add_select_fusion.10
  458.1 1.0 add_select_fusion.10
  464.9 111.7 %all-reduce.15.cloned.1.call-done = f32[1,1,16,16,128]{4,2,3,1,0:T(8,128)} async-done(((f32[1,1,16,16,128]{4,2,3,1,0:T(8,128)}), f32[1,1,16,16,128]{4,2,3,1,0:T(8,128)}) %all-reduce.15.cloned.1.call-update) | async-done | bytes 131088 | tf_op jit(solution)/shard_map/psum | solution.py:48
  576.6 1.0 fusion.337
  577.5 8.0 %collective-permute-start.20 = (bf16[1,16,1,128]{3,1,2,0:T(8,128)(2,1)S(1)}, bf16[1,16,1,128]{3,1,2,0:T(8,128)(2,1)S(1)}, u32[]{:S(2)}, u32[]{:S(2)}) collective-permute-start(bf16[1,16,1,128]{3,1,2,0:T(8,128)(2,1)S(1)} %get-tuple-element.487), channel_id=1, source_target_pairs={{0,1},{1,2},{2,3},{3,4},{4,5},{5,6},{6,7},{8,9},{9,10},{10,11},{11... | collective-permute-start | bytes 12296 | tf_op jit(solution)/shard_map/ppermute | solution.py:22
  585.5 1.9 collective-permute-start.21
  587.9 2.6 collective-permute-done.21
  593.5 1.1 fusion.37
  594.6 2.0 collective-permute-start.22
  596.6 2.4 collective-permute-start.23
  599.3 2.7 collective-permute-done.23
  605.7 1.2 fusion.33
  606.9 1.9 collective-permute-start.24
  608.8 2.6 collective-permute-start.25
  611.6 2.6 collective-permute-done.25
  618.7 75.9 %all-gather.15.cloned.1.call-done = f32[32,1,16,16,128]{4,3,2,1,0:T(8,128)} async-done(((f32[1,1,16,16,128]{4,3,2,1,0:T(8,128)}), f32[32,1,16,16,128]{4,3,2,1,0:T(8,128)}) %all-gather.15.cloned.1.call-update) | async-done | bytes 4194320 | tf_op jit(solution)/shard_map/all_gather | solution.py:30
  694.6 30.2 %while.59 = (s32[]{:T(128)}, f32[1,1,16,16,128]{4,3,2,1,0:T(8,128)S(1)}, s32[]{:T(128)}, f32[32,1,1,16,16,128]{5,4,3,2,1,0:T(8,128)}, s32[]{:T(128)}, /*index=5*/s32[]{:T(128)}) while((s32[]{:T(128)}, f32[1,1,16,16,128]{4,3,2,1,0:T(8,128)S(1)}, s32[]{:T(128)}, f32[32,1,1,16,16,128]{5,4,3,2,1,0:T(8,128)}, s32[]{:T(128)}, ...), condition=%wide.region_14.15_spmd.clone, body=%wide.region_13.14_spmd.clone.sunk | while | flops 98308 | bytes 393309 | solution.py:37
  694.6 1.0 add_select_fusion.11
  (315 shorter events, 164.2 us)
Async XLA Ops:
  6.5 307.3 %copy-start = (f32[5,1,16,16,128]{4,3,2,1,0:T(8,128)S(1)}, f32[5,1,16,16,128]{4,3,2,1,0:T(8,128)}, u32[]{:S(2)}) copy-start(f32[5,1,16,16,128]{4,3,2,1,0:T(8,128)} %param.18) | copy-start | bytes 1966084
  6.5 17.6 %copy-start.6 = (bf16[3,3,192,16]{2,3,1,0:T(8,128)(2,1)S(1)}, bf16[3,3,192,16]{2,3,1,0:T(8,128)(2,1)}, u32[]{:S(2)}) copy-start(bf16[3,3,192,16]{2,3,1,0:T(8,128)(2,1)} %param.20) | copy-start | bytes 165892
  6.5 11.5 %copy-start.8 = (bf16[192,192]{1,0:T(8,128)(2,1)S(1)}, bf16[192,192]{1,0:T(8,128)(2,1)}, u32[]{:S(2)}) copy-start(bf16[192,192]{1,0:T(8,128)(2,1)} %param.23) | copy-start | bytes 221188
  6.5 128.2 %all-gather.9.cloned.1.call-start = ((), (), s32[]{:S(2)}) async-start(), calls=%async_computation.1 | async-start | bytes 4325376 | tf_op jit(solution)/shard_map/all_gather | solution.py:30
  7.6 16.4 %collective-permute-start = (bf16[1,16,1,128]{3,1,2,0:T(8,128)(2,1)S(1)}, bf16[1,16,1,128]{3,1,2,0:T(8,128)(2,1)S(1)}, u32[]{:S(2)}, u32[]{:S(2)}) collective-permute-start(bf16[1,16,1,128]{3,1,2,0:T(8,128)(2,1)S(1)} %get-tuple-element.493), channel_id=1, source_target_pairs={{0,1},{1,2},{2,3},{3,4},{4,5},{5,6},{6,7},{8,9},{9,10},{10,11},{11... | collective-permute-start | bytes 12296 | tf_op jit(solution)/shard_map/ppermute | solution.py:22
  12.2 11.8 %collective-permute-start.1 = (bf16[1,16,1,128]{3,1,2,0:T(8,128)(2,1)S(1)}, bf16[1,16,1,128]{3,1,2,0:T(8,128)(2,1)S(1)}, u32[]{:S(2)}, u32[]{:S(2)}) collective-permute-start(bf16[1,16,1,128]{3,1,2,0:T(8,128)(2,1)S(1)} %get-tuple-element.494), channel_id=1, source_target_pairs={{1,0},{2,1},{3,2},{4,3},{5,4},{6,5},{7,6},{9,8},{10,9},{11,10},{12... | collective-permute-start | bytes 12296 | tf_op jit(solution)/shard_map/ppermute | solution.py:23
  27.1 6.8 copy-start.2
  28.3 6.0 collective-permute-start.2
  32.0 5.4 collective-permute-start.3
  41.1 5.7 copy-start.7
  42.3 4.7 collective-permute-start.4
  44.3 5.4 collective-permute-start.5
  52.1 0.9 copy-start.3
  52.1 1.0 copy-start.5
  54.2 225.1 %all-gather.11.cloned.1.call-start = ((), (), s32[]{:S(2)}) async-start(), calls=%async_computation.2 | async-start | bytes 4325376 | tf_op jit(solution)/shard_map/all_gather | solution.py:30
  165.0 9.6 %collective-permute-start.6 = (bf16[1,16,1,128]{3,1,2,0:T(8,128)(2,1)S(1)}, bf16[1,16,1,128]{3,1,2,0:T(8,128)(2,1)S(1)}, u32[]{:S(2)}, u32[]{:S(2)}) collective-permute-start(bf16[1,16,1,128]{3,1,2,0:T(8,128)(2,1)S(1)} %get-tuple-element.491), channel_id=1, source_target_pairs={{0,1},{1,2},{2,3},{3,4},{4,5},{5,6},{6,7},{8,9},{9,10},{10,11},{11... | collective-permute-start | bytes 12296 | tf_op jit(solution)/shard_map/ppermute | solution.py:22
  172.2 4.9 collective-permute-start.7
  181.3 4.7 collective-permute-start.8
  183.2 5.4 collective-permute-start.9
  193.6 4.8 collective-permute-start.10
  195.5 5.4 collective-permute-start.11
  204.9 229.8 %all-gather.13.cloned.1.call-start = ((), (), s32[]{:S(2)}) async-start(), calls=%async_computation.3 | async-start | bytes 4325376 | tf_op jit(solution)/shard_map/all_gather | solution.py:30
  205.0 151.1 %collective-permute-start.19 = (f32[1,1,16,16,128]{4,2,3,1,0:T(8,128)S(1)}, f32[1,1,16,16,128]{4,2,3,1,0:T(8,128)S(1)}, u32[]{:S(2)}, u32[]{:S(2)}) collective-permute-start(f32[1,1,16,16,128]{4,2,3,1,0:T(8,128)S(1)} %copy.39), channel_id=1, source_target_pairs={{40,0},{48,8},{56,16},{64,24},{72,32},{80,40},{88,48},{96,56},{104... | collective-permute-start | bytes 393224 | tf_op jit(solution)/shard_map/ppermute | solution.py:43
  309.5 6.6 collective-permute-start.12
  316.1 10.7 %collective-permute-start.13 = (bf16[1,16,1,128]{3,1,2,0:T(8,128)(2,1)S(1)}, bf16[1,16,1,128]{3,1,2,0:T(8,128)(2,1)S(1)}, u32[]{:S(2)}, u32[]{:S(2)}) collective-permute-start(bf16[1,16,1,128]{3,1,2,0:T(8,128)(2,1)S(1)} %get-tuple-element.489), channel_id=1, source_target_pairs={{0,1},{1,2},{2,3},{3,4},{4,5},{5,6},{6,7},{8,9},{9,10},{10,11},{11... | collective-permute-start | bytes 12296 | tf_op jit(solution)/shard_map/ppermute | solution.py:22
  324.5 4.9 collective-permute-start.14
  333.6 4.7 collective-permute-start.15
  335.6 5.4 collective-permute-start.16
  345.9 5.0 collective-permute-start.17
  347.8 5.4 collective-permute-start.18
  357.3 219.3 %all-reduce.15.cloned.1.call-start = ((), (), s32[]{:S(2)}) async-start(), calls=%async_computation | async-start | bytes 262144 | tf_op jit(solution)/shard_map/psum | solution.py:48
  358.0 336.6 %all-gather.15.cloned.1.call-start = ((), (), s32[]{:S(2)}) async-start(), calls=%async_computation.4 | async-start | bytes 4325376 | tf_op jit(solution)/shard_map/all_gather | solution.py:30
  577.5 10.3 %collective-permute-start.20 = (bf16[1,16,1,128]{3,1,2,0:T(8,128)(2,1)S(1)}, bf16[1,16,1,128]{3,1,2,0:T(8,128)(2,1)S(1)}, u32[]{:S(2)}, u32[]{:S(2)}) collective-permute-start(bf16[1,16,1,128]{3,1,2,0:T(8,128)(2,1)S(1)} %get-tuple-element.487), channel_id=1, source_target_pairs={{0,1},{1,2},{2,3},{3,4},{4,5},{5,6},{6,7},{8,9},{9,10},{10,11},{11... | collective-permute-start | bytes 12296 | tf_op jit(solution)/shard_map/ppermute | solution.py:22
  585.5 4.9 collective-permute-start.21
  594.6 4.7 collective-permute-start.22
  596.6 5.4 collective-permute-start.23
  606.9 4.7 collective-permute-start.24
  608.8 5.4 collective-permute-start.25
  616.7 0.9 copy-start.4
  694.6 31.1 %copy-start.1 = (f32[5,1,16,16,128]{4,3,2,1,0:T(8,128)S(1)}, f32[5,1,16,16,128]{4,3,2,1,0:T(8,128)}, u32[]{:S(2)}) copy-start(f32[5,1,16,16,128]{4,3,2,1,0:T(8,128)} %param.18) | copy-start | bytes 1966084
Sparse Core Ops, SparseCore 0:
  54.3 80.3 all-gather.8
  205.0 74.1 all-gather.10
  357.4 77.2 all-gather.12
  438.0 138.5 all-reduce.14
  618.8 75.7 all-gather.14
where the time goes:
time: 745 us; the launch traced here: 732 us
  waiting for transfers between devices  448 us (60%)
  other arithmetic  131 us (18%)
  starting transfers between devices  75.3 us (10%)
  matrix products  46.1 us (6%)
  between operations  21.2 us (3%)
  local copies, waits for them, and re-layouts  7.46 us (1%)
    all_gather x4, waiting for transfers between devices, entering_2(): pieces = lax.all_gather(value, axis)  305 us
    select_n x124, other arithmetic, turn(): return jnp.where(position < mine, longer, subtotal)  118 us
    psum x1, waiting for transfers between devices, broadcast(): return lax.psum(kept, axis)  112 us
    dot_general x108, matrix products, convolve(): jnp.einsum('oc,fcrw->forw', weight[row_tap, col_tap], shifted, preferred_...  45.8 us
    ppermute x12, starting transfers between devices, extended(): before = lax.ppermute(last, axis, up)  45.3 us
    ppermute x12, waiting for transfers between devices, extended(): after = lax.ppermute(initial, axis, down)  29 us
    ppermute x12, starting transfers between devices, extended(): after = lax.ppermute(initial, axis, down)  27.3 us
  transfers between devices with their start and end apart: 31, of which 17 were waited for; matrix products, arithmetic and copies ran while one was open for 11% of the time, Pallas kernels for 0%

commit v1 on v0

v1 whole, which is shorter than its diff:
```python
import functools
import jax
import jax.numpy as jnp
from jax import lax
from jax.experimental import pallas as pl
from jax.experimental.pallas import tpu as pltpu
from jax.sharding import PartitionSpec as P

STEPS = 1000
RETIRE = 5
SLOTS = 32
CH = 16
HID = 192
ROWS = 4
COLS = 16
STEP = 3 * CH
BF = jnp.bfloat16
F32 = jnp.float32


def silu(v):
    half = 0.5 * v
    return half + half * jnp.tanh(half)


def sweep_body(sweep, merge, flags, *refs):
    extra = (9, 6, 3, 0)[sweep]
    out_cols = COLS + 2 * extra
    mid_cols, first_cols = out_cols + 2, out_cols + 4
    lanes = -(-out_cols * CH // 128) * 128
    groups_1 = -(-first_cols // 4)
    if sweep == 0:
        x_ref, z_ref, coef, emb, w_in, w_a, w_b, w_c, w_out, low = refs[:10]
        state_out, up_out, down_out = refs[10:13]
    elif sweep == 1:
        u_ref, s_ref, d_ref, x_ref, z_ref, coef, emb, w_in, w_a, w_b, w_c, w_out, low = refs[:13]
        traj_out, state_out, up_out, down_out = refs[13:17]
    elif sweep == 2:
        u_ref, s_ref, d_ref, z_ref, coef, emb, w_in, w_a, w_b, w_c, w_out, low = refs[:12]
        state_out, up_out, down_out = refs[12:15]
    else:
        u_ref, s_ref, d_ref, old_ref, z_ref, coef, emb, w_in, w_a, w_b, w_c, w_out, low = refs[:13]
        traj_out = refs[13]
    hs, f1, f2 = refs[-3:]
    batch = hs.shape[2]

    for y in range(ROWS + 6):
        if sweep == 0:
            row = x_ref[y].astype(BF)
            row = jnp.concatenate([x_ref[y]] * 2, axis=0).astype(BF)
        elif y < 3:
            row = u_ref[y]
        elif y < 3 + ROWS:
            row = s_ref[y - 3].astype(BF)
        else:
            row = d_ref[y - 3 - ROWS]
        for g in range(groups_1):
            hs[g, y] = row[:, 64 * g : 64 * g + 128]

    def stage_1(g, _):
        lhs = jnp.concatenate([hs[g, a : a + ROWS + 4] for a in range(3)], axis=-1)
        lhs = lhs.reshape((ROWS + 4) * batch, 384)
        for ph in range(3):
            acc = jnp.dot(lhs, w_in[ph], preferred_element_type=F32)
            acc = acc.reshape(ROWS + 4, batch, 256)
            if batch < SLOTS:
                acc = jnp.concatenate([acc] * (SLOTS // batch), axis=1)
            acc = silu(acc + emb[ph][None])
            at = pl.multiple_of(768 * g + 256 * ph, 256)
            f1[:, :, pl.ds(at, 256)] = acc.astype(BF)
        return 0

    lax.fori_loop(0, groups_1, stage_1, 0)

    def clear(ref, ahead, height, top, bottom):
        width = ref.shape[2]

        @pl.when(flags[0] == 1)
        def _():
            ref[:, :, 0 : ahead * HID] = jnp.zeros((height, SLOTS, ahead * HID), BF)

        @pl.when(flags[1] == 1)
        def _():
            ref[:, :, (ahead + COLS) * HID :] = jnp.zeros(
                (height, SLOTS, width - (ahead + COLS) * HID), BF
            )

        @pl.when(flags[2] == 1)
        def _():
            ref[0:top] = jnp.zeros((top, SLOTS, width), BF)

        @pl.when(flags[3] == 1)
        def _():
            ref[height - bottom :] = jnp.zeros((bottom, SLOTS, width), BF)

    clear(f1, extra + 2, ROWS + 4, 2, 2)

    mid_rows = ROWS + 2

    def window(g, off, length):
        at = pl.multiple_of(768 * g + off, 128) if not isinstance(g, int) else 768 * g + off
        part = [f1[a : a + mid_rows, :, pl.ds(at, length)] for a in range(3)]
        return jnp.concatenate(part, axis=-1).reshape(mid_rows * SLOTS, 3 * length)

    def put(g, off, acc):
        at = pl.multiple_of(768 * g + off, 128) if not isinstance(g, int) else 768 * g + off
        size = acc.shape[-1]
        f2[:, :, pl.ds(at, size)] = silu(acc).astype(BF).reshape(mid_rows, SLOTS, size)

    groups_2 = mid_cols // 4
    rows_2 = mid_rows * SLOTS

    def stage_2(gs):
        for off, length, shift, w in ((0, 768, 0, w_a), (128, 896, 256, w_b), (384, 768, 512, w_c)):
            lhs = [window(g, off, length) for g in gs]
            lhs = jnp.concatenate(lhs, axis=0) if len(lhs) > 1 else lhs[0]
            acc = jnp.dot(lhs, w[...].reshape(3 * length, 256), preferred_element_type=F32)
            for i, g in enumerate(gs):
                put(g, shift, acc[i * rows_2 : (i + 1) * rows_2])

    def many(i, _):
        stage_2([i * merge + k for k in range(merge)])
        return 0

    lax.fori_loop(0, groups_2 // merge, many, 0)
    rest = groups_2 % merge
    if rest:
        stage_2([groups_2 - rest + k for k in range(rest)])
    if mid_cols % 4:
        g = groups_2
        acc = jnp.dot(
            window(g, 0, 768), w_a[...].reshape(2304, 256), preferred_element_type=F32
        )
        put(g, 0, acc)
        w = jnp.concatenate([w_b[a, 0:640, 0:128] for a in range(3)], axis=0)
        put(g, 256, jnp.dot(window(g, 128, 640), w, preferred_element_type=F32))
    clear(f2, extra + 1, mid_rows, 1, 1)

    full = out_cols // 8
    lhs = [
        jnp.concatenate([f2[a : a + ROWS, :, 1536 * n : 1536 * n + 1920] for a in range(3)], axis=-1)
        .reshape(ROWS * SLOTS, 5760)
        for n in range(full)
    ]
    lhs = jnp.concatenate(lhs, axis=0)
    acc = jnp.dot(lhs, w_out[...].reshape(5760, 128), preferred_element_type=F32)
    acc = acc.reshape(full, ROWS, SLOTS, 128)
    pieces = [acc[n] for n in range(full)]
    left = out_cols - 8 * full
    if left:
        k = (left + 2) * HID
        at = 1536 * full
        lhs = jnp.concatenate([f2[a : a + ROWS, :, at : at + k] for a in range(3)], axis=-1)
        w = jnp.concatenate([w_out[a, 0:k] for a in range(3)], axis=0)
        acc = jnp.dot(lhs.reshape(ROWS * SLOTS, 3 * k), w, preferred_element_type=F32)
        pieces.append(acc.reshape(ROWS, SLOTS, 128))
    predicted = jnp.concatenate(pieces, axis=-1)

    keep = coef[0][:, 0:1]
    predict = coef[1][:, 0:1]
    spread = coef[2][:, 0:1]
    z_at = STEP if sweep in (1, 3) else 0
    where = lax.broadcasted_iota(jnp.int32, (1, lanes), 1)
    low_lane = jnp.where(flags[0] == 1, extra * CH, 0)
    high_lane = jnp.where(flags[1] == 1, (extra + COLS) * CH, lanes)
    inside = jnp.where((where >= low_lane) & (where < high_lane), 1.0, 0.0).astype(F32)
    changes = []
    for y in range(ROWS):
        if sweep == 0:
            now = jnp.concatenate([x_ref[y + 3, :, STEP : STEP + lanes]] * 4, axis=0)
        else:
            now = s_ref[y, :, STEP : STEP + lanes]
        z = z_ref[y, :, z_at : z_at + lanes]
        changes.append(keep * now + predict * predicted[y] + spread * z)
    change = jnp.concatenate(changes, axis=-1)
    total = jnp.dot(low[...], change, preferred_element_type=F32, precision=lax.Precision.HIGHEST)
    for y in range(ROWS):
        if sweep == 0:
            base = x_ref[y + 3, 0:1, STEP : STEP + lanes]
        elif sweep == 1:
            base = x_ref[y + 3, 0:1, 2 * STEP : 2 * STEP + lanes]
        elif sweep == 2:
            base = s_ref[y, 0:1, STEP : STEP + lanes]
        else:
            base = old_ref[y, 0:1, 2 * STEP : 2 * STEP + lanes]
        state = base + total[0:SLOTS, y * lanes : (y + 1) * lanes]
        if sweep == 1:
            traj_out[y] = state[:, 2 * STEP : 2 * STEP + COLS * CH]
            state = base + total[SLOTS:, y * lanes : (y + 1) * lanes]
        if sweep == 3:
            traj_out[y] = state
        else:
            state = state * inside
            state_out[y] = state
            if y < 3:
                up_out[y] = state.astype(BF)
            if y > 0:
                down_out[y - 1] = state.astype(BF)


def sweep_call(sweep, merge, flags, args):
    extra = (9, 6, 3, 0)[sweep]
    out_cols = COLS + 2 * extra
    lanes = -(-out_cols * CH // 128) * 128
    groups_1 = -(-(out_cols + 4) // 4)
    groups_2 = (out_cols + 2) // 4
    f1_lanes = max(groups_1 * 768, (groups_2 - 1) * 768 + 1152)
    shapes = []
    if sweep in (1, 3):
        shapes.append(jax.ShapeDtypeStruct((ROWS, SLOTS, COLS * CH), F32))
    if sweep < 3:
        shapes.append(jax.ShapeDtypeStruct((ROWS, SLOTS, lanes), F32))
        shapes += [jax.ShapeDtypeStruct((3, SLOTS, lanes), BF)] * 2
    vmem = pl.BlockSpec(memory_space=pltpu.VMEM)
    out = pl.pallas_call(
        functools.partial(sweep_body, sweep, merge),
        out_shape=tuple(shapes),
        in_specs=[pl.BlockSpec(memory_space=pltpu.SMEM)] + [vmem] * len(args),
        out_specs=tuple([vmem] * len(shapes)),
        scratch_shapes=[
            pltpu.VMEM((groups_1, ROWS + 6, 16 if sweep == 0 else SLOTS, 128), BF),
            pltpu.VMEM((ROWS + 4, SLOTS, f1_lanes), BF),
            pltpu.VMEM((ROWS + 2, SLOTS, (out_cols + 2) * HID), BF),
        ],
        name=f"sweep{sweep}",
    )(flags, *args)
    return out


def plan_values(sched, time_weight, hidden):
    count = sched.shape[0] - 1
    step = jnp.arange(STEPS)
    betas = 0.0001 + (0.02 - 0.0001) * step.astype(F32) / (STEPS - 1)
    logs = jnp.log(1.0 - betas)[None]
    now, after = sched[:count, None], sched[1:, None]
    log_now = jnp.sum(jnp.where(step[None] <= now, logs, 0.0), axis=1)
    log_after = jnp.sum(jnp.where(step[None] <= after, logs, 0.0), axis=1)
    between = (step[None] <= now) & (step[None] > after)
    retained = jnp.exp(jnp.sum(jnp.where(between, logs, 0.0), axis=1))
    bar_now, bar_after = jnp.exp(log_now), jnp.exp(log_after)
    keep = 1.0 / jnp.sqrt(retained) - 1.0
    predict = -(1.0 - retained) / (jnp.sqrt(1.0 - bar_now) * jnp.sqrt(retained))
    spread = jnp.sqrt((1.0 - bar_after) / (1.0 - bar_now) * (1.0 - retained))
    half = hidden // 2
    freqs = jnp.exp(-9.210340371976184 * jnp.arange(half).astype(F32) / half)
    angles = now.astype(F32) * freqs
    features = jnp.concatenate([jnp.sin(angles), jnp.cos(angles)], axis=-1)
    embedding = jnp.dot(features, time_weight.astype(F32), precision=lax.Precision.HIGHEST)
    return jnp.stack([keep, predict, spread]), embedding


def banded_weights(conv_in, conv_mid, conv_out):
    w = conv_in.transpose(0, 1, 3, 2)
    w_in = jnp.stack([jnp.pad(w, ((0, 0), (p, 5 - p), (0, 0), (0, 0))) for p in range(4)], axis=3)
    w_in = w_in.reshape(3 * 8 * CH, 3, 256).transpose(1, 0, 2)
    w = conv_mid.transpose(0, 1, 3, 2)
    w = jnp.stack([jnp.pad(w, ((0, 0), (p, 3 - p), (0, 0), (0, 0))) for p in range(4)], axis=3)
    w = w.reshape(3, 6 * HID, 4 * HID)
    w_a, w_b, w_c = w[:, 0:768, 0:256], w[:, 128:1024, 256:512], w[:, 384:1152, 512:768]
    w = conv_out.transpose(0, 1, 3, 2)
    w = jnp.stack([jnp.pad(w, ((0, 0), (p, 7 - p), (0, 0), (0, 0))) for p in range(8)], axis=3)
    w_out = w.reshape(3, 10 * HID, 8 * CH)
    return [w_in, w_a, w_b, w_c, w_out]


def shards(x_start, noise, fresh, sched, conv_in, conv_mid, conv_out, time_weight):
    column_parts, row_parts = 128 // COLS, 16 // ROWS
    strips = lax.axis_size("rows")
    slot, strip = lax.axis_index("tm"), lax.axis_index("rows")
    column, quarter = slot // row_parts, slot % row_parts

    down, up = [], []
    for c in range(column_parts):
        place = [(c * row_parts + k % row_parts) * strips + k // row_parts for k in range(strips * row_parts)]
        down += list(zip(place[:-1], place[1:]))
        up += list(zip(place[1:], place[:-1]))

    def rim(for_upper, for_lower):
        below = lax.ppermute(for_upper, ("tm", "rows"), up)
        above = lax.ppermute(for_lower, ("tm", "rows"), down)
        return above, below

    strip_up = [(i + 1, i) for i in range(strips - 1)]
    strip_down = [(i, i + 1) for i in range(strips - 1)]
    latent = x_start[0]
    above = lax.ppermute(latent[:, 13:16].astype(BF), "rows", strip_down)
    below = lax.ppermute(latent[:, 0:3].astype(BF), "rows", strip_up)

    z = noise[0, 0].transpose(1, 2, 0)
    high = lax.reduce_precision(z, 8, 7)
    low_half = (z - high).astype(BF).reshape(16, column_parts, COLS * CH)
    high = jnp.pad(high.astype(BF), ((0, 0), (9, 9), (0, 0))).reshape(16, 146 * CH)
    parts = []
    for c in range(column_parts):
        parts.append(
            jnp.concatenate(
                [high[:, 256 * c : 256 * c + 544], low_half[:, c], jnp.zeros((16, 224), BF)], axis=-1
            )
        )
    sent = jnp.stack(parts).reshape(SLOTS, ROWS * 8, 128)
    got = lax.all_to_all(sent, "tm", 0, 0, tiled=True)
    got = got.reshape(SLOTS, ROWS, 1024).transpose(1, 0, 2)
    z9 = jnp.pad(got[:, :, 0:544].astype(F32), ((0, 0), (0, 0), (0, 96)))
    z9 = z9 + jnp.pad(got[:, :, 544:800].astype(F32), ((0, 0), (0, 0), (144, 240)))

    weights = banded_weights(conv_in, conv_mid, conv_out)
    values, embedding = plan_values(sched, time_weight, HID)

    def coefs(r):
        mine = values[:, RETIRE * r : RETIRE * r + SLOTS]
        table = jnp.broadcast_to(mine[:, :, None], (3, SLOTS, 128))
        emb = jnp.tile(embedding[RETIRE * r : RETIRE * r + SLOTS], (1, 4))
        return table, emb.reshape(SLOTS, 3, 256).transpose(1, 0, 2)

    i, j = jnp.arange(SLOTS)[None], jnp.arange(SLOTS)[:, None]
    low = (i < j).astype(F32)
    moved = jnp.where(j < SLOTS - RETIRE, j + RETIRE, j)
    low_2 = jnp.concatenate([low, (i < moved).astype(F32)])

    flags = jnp.stack(
        [
            column == 0,
            column == column_parts - 1,
            (strip == 0) & (quarter == 0),
            (strip == strips - 1) & (quarter == row_parts - 1),
        ]
    ).astype(jnp.int32)

    f = fresh[:, 0].transpose(2, 0, 3, 1)
    f = jnp.pad(f, ((0, 0), (0, 0), (3, 5), (0, 0))).reshape(16, RETIRE, 136 * CH)
    f = lax.dynamic_slice(f, (quarter * ROWS, 0, column * 256), (ROWS, RETIRE, 384))
    lane = jnp.arange(384)
    f = jnp.where(lane < 352, f, 0.0)
    z3 = jnp.concatenate([z9[:, RETIRE:, 96:480], f], axis=1)

    x = jnp.concatenate([above.astype(F32), latent, below.astype(F32)], axis=1)
    x = jnp.pad(x.transpose(1, 2, 0), ((0, 0), (12, 20), (0, 0))).reshape(22, 160 * CH)
    x = lax.dynamic_slice(x, (quarter * ROWS, column * 256), (ROWS + 6, 768))
    x = jnp.broadcast_to(x[:, None], (ROWS + 6, 8, 768))

    table, emb = coefs(0)
    s1, to_upper, to_lower = sweep_call(0, MERGE, flags, [x, z9, table, emb, *weights, low])
    above, below = rim(to_upper, to_lower)
    first_out, s2, to_upper, to_lower = sweep_call(
        1, MERGE, flags, [above, s1, below, x, z9, table, emb, *weights, low_2]
    )
    above, below = rim(to_upper, to_lower)
    table, emb = coefs(1)
    s3, to_upper, to_lower = sweep_call(
        2, MERGE, flags, [above, s2, below, z3, table, emb, *weights, low]
    )
    above, below = rim(to_upper, to_lower)
    (second_out,) = sweep_call(
        3, MERGE, flags, [above, s3, below, s2, z3, table, emb, *weights, low]
    )
    out = jnp.stack([first_out, second_out]).transpose(2, 0, 1, 3).reshape(SLOTS, 16, 128)
    out = lax.all_to_all(out, "tm", 0, 0, tiled=True)
    out = out.reshape(column_parts, row_parts, 2, ROWS, COLS, CH).transpose(2, 5, 1, 3, 0, 4)
    return out.reshape(2, 1, 1, CH, 16, 128)


MERGE = 2


def solution(mesh):
    placed = (
        P(None, None, "rows", None),
        P("tm", None, None, "rows", None),
        P(None, None, None, "rows", None),
        P(),
        P(),
        P(),
        P(),
        P(),
    )
    return jax.shard_map(
        shards,
        mesh=mesh,
        in_specs=placed,
        out_specs=P(None, "tm", None, None, "rows", None),
        check_vma=False,
    )
```

time: 745 us -> 225 us (0.30); the launches traced: 732 us -> 221 us
  waiting for transfers between devices: 448 us -> 6.62 us
  other arithmetic: 131 us -> 11.6 us
  local copies, waits for them, and re-layouts: 7.46 us -> 77.3 us
  Pallas kernels: 0 us -> 63 us
  matrix products: 46.1 us -> 0.24 us
  starting transfers between devices: 75.3 us -> 38.2 us
  blocking collectives: 0 us -> 22.8 us
  between operations: 21.2 us -> 1.07 us
    all_gather x4 -> x0, waiting for transfers between devices: 305 us -> none  [entering_2(): pieces = lax.all_gather(value, axis)]
    select_n x125 -> x2, other arithmetic: 119 us -> 0.02 us  [the longest x1 0.02 us: shards(): f = jnp.where(lane < 352, f, 0.0)]
    psum x1 -> x0, waiting for transfers between devices: 112 us -> none  [broadcast(): return lax.psum(kept, axis)]
    pallas_call x0 -> x4, Pallas kernels: none -> 63 us  [sweep_call(): pl.pallas_call(functools.partial(sweep_body, sweep, merge), out_shape=tup...]
    ppermute x26 -> x8, starting transfers between devices: 75.2 us -> 26.8 us  [the longest x3 11 us: rim(): above = lax.ppermute(for_lower, ('tm', 'rows'), down)]
    dot_general x110 -> x1, matrix products: 46.1 us -> 0.24 us  [plan_values(): jnp.dot(features, time_weight.astype(F32), precision=lax.Precision.HIGHEST)]
    reshape x1 -> x15, local copies, waits for them, and re-layouts: 0.01 us -> 32.6 us  [the longest x1 12.8 us: banded_weights(): w = w.reshape(3, 6 * HID, 4 * HID)]
    ppermute x26 -> x8, waiting for transfers between devices: 31.2 us -> 6.61 us  [the longest x3 6.3 us: rim(): below = lax.ppermute(for_upper, ('tm', 'rows'), up)]
  transfers between devices with their start and end apart: 31 -> 9, of which waited for: 17 -> 4; matrix products, arithmetic and copies ran while one was open for 11% -> 34% of each run, Pallas kernels for 0% -> 0%
where the time goes in v1:
time: 225 us; the launch traced here: 221 us
  local copies, waits for them, and re-layouts  77.3 us (34%)
  Pallas kernels  63 us (28%)
  starting transfers between devices  38.2 us (17%)
  blocking collectives  22.8 us (10%)
  other arithmetic  11.6 us (5%)
  waiting for transfers between devices  6.62 us (3%)
    pallas_call x4, Pallas kernels, sweep_call(): pl.pallas_call(functools.partial(sweep_body, sweep, merge), out_shape=tup...  63 us
    all_to_all x1, blocking collectives, shards(): out = lax.all_to_all(out, 'tm', 0, 0, tiled=True)  22.8 us
    another operation x2, local copies, waits for them, and re-layouts, banded_weights(): jnp.stack([jnp.pad(w, ((0, 0), (p, 3 - p), (0, 0), (0, 0))) for p in rang...  14.8 us
    reshape x1, local copies, waits for them, and re-layouts, banded_weights(): w = w.reshape(3, 6 * HID, 4 * HID)  12.8 us
    all_to_all x1, starting transfers between devices, shards(): got = lax.all_to_all(sent, 'tm', 0, 0, tiled=True)  11.3 us
    ppermute x3, starting transfers between devices, rim(): above = lax.ppermute(for_lower, ('tm', 'rows'), down)  11 us
    ppermute x3, starting transfers between devices, rim(): below = lax.ppermute(for_upper, ('tm', 'rows'), up)  9.33 us
    unnamed x50, local copies, waits for them, and re-layouts  6.69 us
  transfers between devices with their start and end apart: 9, of which 4 were waited for; matrix products, arithmetic and copies ran while one was open for 34% of the time, Pallas kernels for 0%

profile of v1, /device:TPU:1, one launch (start us, length us, event | category | flops | bytes accessed | tf_op | source)
XLA Modules:
  0.0 220.7 jit_solution(13281120072573787290)
XLA Ops:
  0.0 0.9 bitcast_convert_fusion
  1.0 4.6 %collective-permute-start = (bf16[16,3,128]{2,1,0:T(4,128)(2,1)S(1)}, bf16[16,3,128]{2,1,0:T(4,128)(2,1)S(1)}, u32[]{:S(2)}, u32[]{:S(2)}) collective-permute-start(bf16[16,3,128]{2,1,0:T(4,128)(2,1)S(1)} %get-tuple-element.56), channel_id=1, source_target_pairs={{0,1},{1,2},{2,3},{3,4},{4,5},{5,6},{6,7},{8,9},{9,10},{10,11},{11... | collective-permute-start | bytes 36872 | tf_op jit(solution)/shard_map/ppermute | solution.py:286
  5.6 1.9 collective-permute-start.1
  7.5 0.9 reduce-precision_convert_fusion
  8.4 0.3 copy.102
  8.9 0.4 reshape.169
  9.4 0.3 copy.66
  9.7 0.5 reshape.170
  11.0 0.8 reshape.171
  11.9 11.3 %all-to-all-start = ((bf16[32,32,128]{2,1,0:T(8,128)(2,1)}), bf16[32,32,128]{2,1,0:T(8,128)(2,1)}, u32[]{:S(2)}, u32[]{:S(2)}) async-start(bf16[32,32,128]{2,1,0:T(8,128)(2,1)} %reshape.171), calls=%async_computation | async-start | bytes 524288 | tf_op jit(solution)/shard_map/all_to_all | solution.py:301
  23.3 0.6 fusion.6.refs_9_.refs_11_.refs_12_
  24.0 0.2 select_reduce_fusion.2
  24.5 0.2 fusion.2
  24.8 0.7 pad_bitcast_fusion.7
  25.7 1.3 copy-done.4
  27.0 3.2 %copy.103 = f32[16,5,128,16]{3,2,1,0:T(8,128)} copy(f32[16,5,128,16]{2,0,3,1:T(8,128)S(1)} %bitcast.150) | data formatting | bytes 1310720
  30.2 5.6 %pad.112.clone = f32[16,5,136,16]{3,2,1,0:T(8,128)} pad(f32[16,5,128,16]{3,2,1,0:T(8,128)} %copy.103, f32[]{:T(128)} %constant.65.clone.1), padding=0_0x0_0x3_5x0_0 | pad | bytes 1351684 | tf_op jit(solution)/shard_map/jit(_pad)/pad | solution.py:330
  35.8 4.4 %reshape.182 = f32[16,5,2176]{2,1,0:T(8,128)S(1)} reshape(f32[16,5,136,16]{3,2,1,0:T(8,128)} %pad.112.clone) | data formatting | bytes 1392640 | tf_op jit(solution)/shard_map/reshape | solution.py:330
  40.1 0.8 pad_bitcast_fusion.3
  41.0 4.0 %pad_maximum_fusion = bf16[3,6,192,4,192]{2,4,1,0,3:T(8,128)(2,1)} fusion(bf16[3,6,192,1,192]{2,4,1,0,3:T(8,128)(2,1)S(1)} %get-tuple-element.31, bf16[3,6,192,1,192]{2,4,1,0,3:T(8,128)(2,1)S(1)} %get-tuple-element.32, bf16[3,6,192,1,192]{2,4,1,0,3:T(8,128)(2,1)S(1)} %get-tuple-element.33, bf16[3,6,192,1,192]{2,4,1,0,3:T(8,128)(2,1)S(1)} %get-tuple-element.30), kind=kLoop, calls=%fused_computation | loop fusion | flops 7962624 | bytes 10616832 | tf_op jit(solution)/shard_map/stack | solution.py:257
  45.0 13.9 %copy.79 = bf16[3,6,192,4,192]{4,3,2,1,0:T(4,128)(2,1)} copy(bf16[3,6,192,4,192]{2,4,1,0,3:T(8,128)(2,1)} %pad_maximum_fusion) | data formatting | bytes 10616832 | tf_op jit(solution)/shard_map/stack | solution.py:257
  58.9 12.8 %reshape.174 = bf16[3,1152,768]{2,1,0:T(8,128)(2,1)} reshape(bf16[3,6,192,4,192]{4,3,2,1,0:T(4,128)(2,1)} %copy.79) | data formatting | bytes 10616832 | tf_op jit(solution)/shard_map/reshape | solution.py:258
  71.9 3.2 %fusion.10 = (bf16[3,768,256]{2,1,0:T(8,128)(2,1)}, bf16[3,768,256]{2,1,0:T(8,128)(2,1)}) fusion(bf16[3,1152,768]{2,1,0:T(8,128)(2,1)} %reshape.174), kind=kLoop, calls=%fused_computation.87 | loop fusion | bytes 4718592 | tf_op jit(solution)/shard_map/slice | solution.py:259
  75.1 0.7 add_convert_fusion.flags
  75.8 2.6 %slice.145.refs_6_.refs_9_.refs_8_ = bf16[3,896,256]{2,1,0:T(8,128)(2,1)} slice(bf16[3,1152,768]{2,1,0:T(8,128)(2,1)} %reshape.174), slice={[0:3], [128:1024], [256:512]} | slice | bytes 2752512 | tf_op jit(solution)/shard_map/slice | solution.py:259
  78.5 0.6 copy.119
  79.2 0.6 copy.77
  79.8 1.0 reshape.173
  80.8 0.9 copy.116
  81.7 2.6 %copy.80 = bf16[3,10,192,8,16]{2,1,4,3,0:T(8,128)(2,1)S(1)} copy(bf16[3,10,192,8,16]{2,4,1,0,3:T(8,128)(2,1)} %copy-done.4) | data formatting | bytes 2949120 | tf_op jit(solution)/shard_map/stack | solution.py:261
  84.3 3.3 %reshape.175 = bf16[3,1920,128]{1,2,0:T(8,128)(2,1)} reshape(bf16[3,10,192,8,16]{2,1,4,3,0:T(8,128)(2,1)S(1)} %copy.80) | data formatting | bytes 2949120 | tf_op jit(solution)/shard_map/reshape | solution.py:262
  87.6 2.8 %copy.81.refs_8_.refs_11_.refs_10_ = bf16[3,1920,128]{2,1,0:T(8,128)(2,1)} copy(bf16[3,1920,128]{1,2,0:T(8,128)(2,1)} %reshape.175) | data formatting | bytes 2949120 | tf_op jit(solution)/shard_map/reshape | solution.py:262
  90.4 0.4 copy.101
  90.9 0.2 pad.90.clone
  91.2 1.3 reshape.168
  92.5 1.0 reshape.172
  93.7 0.8 convert_add_fusion.refs_1_.refs_4_
  94.6 0.7 broadcast_in_dim.63.refs_2_.refs_5_
  95.2 0.7 broadcast_in_dim.60.refs_0_.refs_3_
  96.0 19.2 %sweep0.1 = (f32[4,32,640]{2,1,0:T(8,128)}, bf16[3,32,640]{2,1,0:T(8,128)(2,1)}, bf16[3,32,640]{2,1,0:T(8,128)(2,1)}) custom-call(s32[4]{0:T(128)} %add_convert_fusion.flags, f32[10,8,768]{2,1,0:T(8,128)} %broadcast_in_dim.60.refs_0_.refs_3_, f32[4,32,640]{2,1,0:T(8,128)} %convert_add_fusion.refs_1_.refs_4_, f32[3,32,128]{2,1,0:T(8,128)} %broadcast_in_dim.63.refs_2_.refs_5_, ...), custom_call_target="tpu_custom_call" | custom-call | tf_op jit(solution)/shard_map/sweep0/pallas_call | solution.py:215
  115.2 3.2 %collective-permute-start.2 = (bf16[3,32,640]{2,1,0:T(8,128)(2,1)}, bf16[3,32,640]{2,1,0:T(8,128)(2,1)S(1)}, u32[]{:S(2)}, u32[]{:S(2)}) collective-permute-start(bf16[3,32,640]{2,1,0:T(8,128)(2,1)} %get-tuple-element.15), channel_id=1, source_target_pairs={{0,8},{8,16},{16,24},{24,1},{1,9},{9,17},{17,25},{25,2},{2,10},{10... | collective-permute-start | bytes 368648 | tf_op jit(solution)/shard_map/ppermute | solution.py:280
  118.4 3.5 %collective-permute-start.3 = (bf16[3,32,640]{2,1,0:T(8,128)(2,1)}, bf16[3,32,640]{2,1,0:T(8,128)(2,1)S(1)}, u32[]{:S(2)}, u32[]{:S(2)}) collective-permute-start(bf16[3,32,640]{2,1,0:T(8,128)(2,1)} %get-tuple-element.17), channel_id=1, source_target_pairs={{8,0},{16,8},{24,16},{1,24},{9,1},{17,9},{25,17},{2,25},{10,2},{18... | collective-permute-start | bytes 368648 | tf_op jit(solution)/shard_map/ppermute | solution.py:279
  122.2 0.7 copy.118
  122.9 0.6 pad_maximum_fusion.3.refs_12_
  123.7 1.3 collective-permute-done.3.refs_2_
  124.9 0.7 copy-done.12
  125.6 18.0 %sweep1.1 = (f32[4,32,256]{2,1,0:T(8,128)}, f32[4,32,512]{2,1,0:T(8,128)}, bf16[3,32,512]{2,1,0:T(8,128)(2,1)}, bf16[3,32,512]{2,1,0:T(8,128)(2,1)}) custom-call(s32[4]{0:T(128)} %add_convert_fusion.flags, bf16[3,32,640]{2,1,0:T(8,128)(2,1)} %copy-done.11, f32[4,32,640]{2,1,0:T(8,128)} %get-tuple-element.16.refs_1_, bf16[3,32,640]{2,1,0:T(8,128)(2,1)} %copy-done.12, ...), custom_call_target="tpu_custom_call" | custom-call | tf_op jit(solution)/shard_map/sweep1/pallas_call | solution.py:215
  143.6 3.1 %collective-permute-start.4 = (bf16[3,32,512]{2,1,0:T(8,128)(2,1)}, bf16[3,32,512]{2,1,0:T(8,128)(2,1)S(1)}, u32[]{:S(2)}, u32[]{:S(2)}) collective-permute-start(bf16[3,32,512]{2,1,0:T(8,128)(2,1)} %get-tuple-element.19), channel_id=1, source_target_pairs={{0,8},{8,16},{16,24},{24,1},{1,9},{9,17},{17,25},{25,2},{2,10},{10... | collective-permute-start | bytes 294920 | tf_op jit(solution)/shard_map/ppermute | solution.py:280
  146.6 3.7 %collective-permute-start.5 = (bf16[3,32,512]{2,1,0:T(8,128)(2,1)}, bf16[3,32,512]{2,1,0:T(8,128)(2,1)S(1)}, u32[]{:S(2)}, u32[]{:S(2)}) collective-permute-start(bf16[3,32,512]{2,1,0:T(8,128)(2,1)} %get-tuple-element.21), channel_id=1, source_target_pairs={{8,0},{16,8},{24,16},{1,24},{9,1},{17,9},{25,17},{2,25},{10,2},{18... | collective-permute-start | bytes 294920 | tf_op jit(solution)/shard_map/ppermute | solution.py:279
  150.3 0.7 pad_maximum_fusion.2.refs_3_.refs_4_
  151.0 1.8 collective-permute-done.5.refs_2_
  152.8 0.7 broadcast_in_dim.66.refs_4_.refs_5_
  153.5 14.1 %sweep2.1 = (f32[4,32,384]{2,1,0:T(8,128)}, bf16[3,32,384]{2,1,0:T(8,128)(2,1)}, bf16[3,32,384]{2,1,0:T(8,128)(2,1)}) custom-call(s32[4]{0:T(128)} %add_convert_fusion.flags, bf16[3,32,512]{2,1,0:T(8,128)(2,1)} %copy-done.13, f32[4,32,512]{2,1,0:T(8,128)} %get-tuple-element.20.refs_1_.refs_3_, bf16[3,32,512]{2,1,0:T(8,128)(2,1)} %copy-done.14, ...), custom_call_target="tpu_custom_call" | custom-call | tf_op jit(solution)/shard_map/sweep2/pallas_call | solution.py:215
  167.6 4.7 %collective-permute-start.6 = (bf16[3,32,384]{2,1,0:T(8,128)(2,1)}, bf16[3,32,384]{2,1,0:T(8,128)(2,1)S(1)}, u32[]{:S(2)}, u32[]{:S(2)}) collective-permute-start(bf16[3,32,384]{2,1,0:T(8,128)(2,1)} %get-tuple-element.22), channel_id=1, source_target_pairs={{0,8},{8,16},{16,24},{24,1},{1,9},{9,17},{17,25},{25,2},{2,10},{10... | collective-permute-start | bytes 221192 | tf_op jit(solution)/shard_map/ppermute | solution.py:280
  172.3 2.1 collective-permute-start.7
  174.4 0.3 collective-permute-done.6.refs_0_
  174.7 3.3 %collective-permute-done.7.refs_2_ = bf16[3,32,384]{2,1,0:T(8,128)(2,1)S(1)} collective-permute-done((bf16[3,32,384]{2,1,0:T(8,128)(2,1)}, bf16[3,32,384]{2,1,0:T(8,128)(2,1)S(1)}, u32[]{:S(2)}, u32[]{:S(2)}) %collective-permute-start.7) | collective-permute-done | bytes 73760 | tf_op jit(solution)/shard_map/ppermute | solution.py:279
  178.0 0.6 copy-done.17
  178.7 11.6 %sweep3.1 = f32[4,32,256]{2,1,0:T(8,128)} custom-call(s32[4]{0:T(128)} %add_convert_fusion.flags, bf16[3,32,384]{2,1,0:T(8,128)(2,1)} %copy-done.16, f32[4,32,384]{2,1,0:T(8,128)} %get-tuple-element.23.refs_1_, bf16[3,32,384]{2,1,0:T(8,128)(2,1)} %copy-done.17, f32[4,32,512]{2,1,0:T(8,128)} %get-tuple-element.20.refs_1_.refs_3_, ...), custom_call_target="tpu_custom_call" | custom-call | tf_op jit(solution)/shard_map/sweep3/pallas_call | solution.py:215
  190.3 0.9 maximum_bitcast_fusion
  191.5 22.8 %all_to_all.10 = f32[32,16,128]{2,1,0:T(8,128)S(1)} all-to-all(f32[32,16,128]{2,1,0:T(8,128)S(1)} %reshape.177), channel_id=1, replica_groups=mesh['tm'=32,'rows'=8] {'tm'}, dimensions={0} | all-to-all | bytes 524288 | tf_op jit(solution)/shard_map/all_to_all | solution.py:357
  214.3 0.6 reshape.178
  214.9 2.6 %copy.89 = f32[2,16,4,4,8,16]{5,4,3,2,1,0:T(8,128)} copy(f32[2,16,4,4,8,16]{1,5,3,0,2,4:T(8,128)S(1)} %bitcast.134) | data formatting | bytes 524288 | tf_op jit(solution)/shard_map/transpose | solution.py:358
  217.5 2.8 %reshape.179 = f32[2,1,1,16,16,128]{5,4,3,0,2,1:T(8,128)} reshape(f32[2,16,4,4,8,16]{5,4,3,2,1,0:T(8,128)} %copy.89) | data formatting | bytes 524288 | tf_op jit(solution)/shard_map/reshape | solution.py:359
  (94 shorter events, 3.0 us)
Async XLA Ops:
  0.0 24.5 %copy-start = (bf16[192,192]{1,0:T(8,128)(2,1)S(1)}, bf16[192,192]{1,0:T(8,128)(2,1)}, u32[]{:S(2)}) copy-start(bf16[192,192]{1,0:T(8,128)(2,1)} %param.15) | copy-start | bytes 221188
  1.0 89.4 %collective-permute-start = (bf16[16,3,128]{2,1,0:T(4,128)(2,1)S(1)}, bf16[16,3,128]{2,1,0:T(4,128)(2,1)S(1)}, u32[]{:S(2)}, u32[]{:S(2)}) collective-permute-start(bf16[16,3,128]{2,1,0:T(4,128)(2,1)S(1)} %get-tuple-element.56), channel_id=1, source_target_pairs={{0,1},{1,2},{2,3},{3,4},{4,5},{5,6},{6,7},{8,9},{9,10},{10,11},{11... | collective-permute-start | bytes 36872 | tf_op jit(solution)/shard_map/ppermute | solution.py:286
  5.6 84.8 %collective-permute-start.1 = (bf16[16,3,128]{2,1,0:T(4,128)(2,1)S(1)}, bf16[16,3,128]{2,1,0:T(4,128)(2,1)S(1)}, u32[]{:S(2)}, u32[]{:S(2)}) collective-permute-start(bf16[16,3,128]{2,1,0:T(4,128)(2,1)S(1)} %get-tuple-element.57), channel_id=1, source_target_pairs={{1,0},{2,1},{3,2},{4,3},{5,4},{6,5},{7,6},{9,8},{10,9},{11,10},{12... | collective-permute-start | bytes 36872 | tf_op jit(solution)/shard_map/ppermute | solution.py:287
  9.3 14.6 %copy-start.18 = (s32[38]{0:T(128)S(1)}, s32[38]{0:T(128)}, u32[]{:S(2)}) copy-start(s32[38]{0:T(128)} %param.11) | copy-start | bytes 460
  9.3 15.4 %copy-start.15 = (bf16[3,3,192,16]{2,3,1,0:T(8,128)(2,1)S(1)}, bf16[3,3,192,16]{2,3,1,0:T(8,128)(2,1)}, u32[]{:S(2)}) copy-start(bf16[3,3,192,16]{2,3,1,0:T(8,128)(2,1)} %param.12) | copy-start | bytes 165892
  9.7 15.8 %copy-start.2 = (bf16[3,3,16,192]{3,2,1,0:T(8,128)(2,1)S(1)}, bf16[3,3,16,192]{3,2,1,0:T(8,128)(2,1)}, u32[]{:S(2)}) copy-start(bf16[3,3,16,192]{3,2,1,0:T(8,128)(2,1)} %param.14) | copy-start | bytes 165892
  11.9 80.7 %all-to-all-start = ((bf16[32,32,128]{2,1,0:T(8,128)(2,1)}), bf16[32,32,128]{2,1,0:T(8,128)(2,1)}, u32[]{:S(2)}, u32[]{:S(2)}) async-start(bf16[32,32,128]{2,1,0:T(8,128)(2,1)} %reshape.171), calls=%async_computation | async-start | bytes 524288 | tf_op jit(solution)/shard_map/all_to_all | solution.py:301
  23.2 3.8 %copy-start.7 = (f32[5,1,16,16,128]{4,3,2,1,0:T(8,128)S(1)}, f32[5,1,16,16,128]{4,3,2,1,0:T(8,128)}, u32[]{:S(2)}) copy-start(f32[5,1,16,16,128]{4,3,2,1,0:T(8,128)} %param.10) | copy-start | bytes 1966084
  25.7 1.3 copy-start.4
  35.8 4.4 %copy-start.5 = (bf16[3,3,192,192]{3,2,1,0:T(8,128)(2,1)S(1)}, bf16[3,3,192,192]{3,2,1,0:T(8,128)(2,1)}, u32[]{:S(2)}) copy-start(bf16[3,3,192,192]{3,2,1,0:T(8,128)(2,1)} %param.13) | copy-start | bytes 1990660
  58.9 12.8 %copy-start.6 = (bf16[3,8,16,1,192]{4,2,1,0,3:T(8,128)(2,1)S(1)}, bf16[3,8,16,1,192]{4,2,1,0,3:T(8,128)(2,1)}, u32[]{:S(2)}) copy-start(bf16[3,8,16,1,192]{4,2,1,0,3:T(8,128)(2,1)} %get-tuple-element.47) | copy-start | bytes 442372
  87.6 2.8 %copy-start.8 = (f32[1,16,16,128]{3,2,1,0:T(8,128)S(1)}, f32[1,16,16,128]{3,2,1,0:T(8,128)}, u32[]{:S(2)}) copy-start(f32[1,16,16,128]{3,2,1,0:T(8,128)} %param.8) | copy-start | bytes 393220
  91.1 2.6 %copy-start.19 = (pred[640]{0:T(1024)(128)(4,1)S(1)}, pred[640]{0:T(1024)(128)(4,1)}, u32[]{:S(2)}) copy-start(pred[640]{0:T(1024)(128)(4,1)} %constant.69.clone.1) | copy-start | bytes 1924
  96.0 26.9 %copy-start.9 = (f32[32,32]{1,0:T(8,128)S(1)}, f32[32,32]{1,0:T(8,128)}, u32[]{:S(2)}) copy-start(f32[32,32]{1,0:T(8,128)} %fusion.6.refs_9_.refs_11_.refs_12_) | copy-start | bytes 12292
  96.0 27.6 %copy-start.3 = (f32[4,32,640]{2,1,0:T(8,128)S(1)}, f32[4,32,640]{2,1,0:T(8,128)}, u32[]{:S(2)}) copy-start(f32[4,32,640]{2,1,0:T(8,128)} %convert_add_fusion.refs_1_.refs_4_) | copy-start | bytes 983044
  115.2 8.4 %collective-permute-start.2 = (bf16[3,32,640]{2,1,0:T(8,128)(2,1)}, bf16[3,32,640]{2,1,0:T(8,128)(2,1)S(1)}, u32[]{:S(2)}, u32[]{:S(2)}) collective-permute-start(bf16[3,32,640]{2,1,0:T(8,128)(2,1)} %get-tuple-element.15), channel_id=1, source_target_pairs={{0,8},{8,16},{16,24},{24,1},{1,9},{9,17},{17,25},{25,2},{2,10},{10... | collective-permute-start | bytes 368648 | tf_op jit(solution)/shard_map/ppermute | solution.py:280
  118.4 6.5 %collective-permute-start.3 = (bf16[3,32,640]{2,1,0:T(8,128)(2,1)}, bf16[3,32,640]{2,1,0:T(8,128)(2,1)S(1)}, u32[]{:S(2)}, u32[]{:S(2)}) collective-permute-start(bf16[3,32,640]{2,1,0:T(8,128)(2,1)} %get-tuple-element.17), channel_id=1, source_target_pairs={{8,0},{16,8},{24,16},{1,24},{9,1},{17,9},{25,17},{2,25},{10,2},{18... | collective-permute-start | bytes 368648 | tf_op jit(solution)/shard_map/ppermute | solution.py:279
  123.6 1.3 copy-start.11
  124.9 0.7 copy-start.12
  143.6 7.5 %collective-permute-start.4 = (bf16[3,32,512]{2,1,0:T(8,128)(2,1)}, bf16[3,32,512]{2,1,0:T(8,128)(2,1)S(1)}, u32[]{:S(2)}, u32[]{:S(2)}) collective-permute-start(bf16[3,32,512]{2,1,0:T(8,128)(2,1)} %get-tuple-element.19), channel_id=1, source_target_pairs={{0,8},{8,16},{16,24},{24,1},{1,9},{9,17},{17,25},{25,2},{2,10},{10... | collective-permute-start | bytes 294920 | tf_op jit(solution)/shard_map/ppermute | solution.py:280
  146.6 6.2 %collective-permute-start.5 = (bf16[3,32,512]{2,1,0:T(8,128)(2,1)}, bf16[3,32,512]{2,1,0:T(8,128)(2,1)S(1)}, u32[]{:S(2)}, u32[]{:S(2)}) collective-permute-start(bf16[3,32,512]{2,1,0:T(8,128)(2,1)} %get-tuple-element.21), channel_id=1, source_target_pairs={{8,0},{16,8},{24,16},{1,24},{9,1},{17,9},{25,17},{2,25},{10,2},{18... | collective-permute-start | bytes 294920 | tf_op jit(solution)/shard_map/ppermute | solution.py:279
  151.0 2.4 %copy-start.13 = (bf16[3,32,512]{2,1,0:T(8,128)(2,1)}, bf16[3,32,512]{2,1,0:T(8,128)(2,1)S(1)}, u32[]{:S(2)}) copy-start(bf16[3,32,512]{2,1,0:T(8,128)(2,1)S(1)} %collective-permute-done.4.refs_0_) | copy-start | bytes 294916
  152.8 0.7 copy-start.14
  167.6 7.1 %collective-permute-start.6 = (bf16[3,32,384]{2,1,0:T(8,128)(2,1)}, bf16[3,32,384]{2,1,0:T(8,128)(2,1)S(1)}, u32[]{:S(2)}, u32[]{:S(2)}) collective-permute-start(bf16[3,32,384]{2,1,0:T(8,128)(2,1)} %get-tuple-element.22), channel_id=1, source_target_pairs={{0,8},{8,16},{16,24},{24,1},{1,9},{9,17},{17,25},{25,2},{2,10},{10... | collective-permute-start | bytes 221192 | tf_op jit(solution)/shard_map/ppermute | solution.py:280
  172.3 5.7 %collective-permute-start.7 = (bf16[3,32,384]{2,1,0:T(8,128)(2,1)}, bf16[3,32,384]{2,1,0:T(8,128)(2,1)S(1)}, u32[]{:S(2)}, u32[]{:S(2)}) collective-permute-start(bf16[3,32,384]{2,1,0:T(8,128)(2,1)} %get-tuple-element.24), channel_id=1, source_target_pairs={{8,0},{16,8},{24,16},{1,24},{9,1},{17,9},{25,17},{2,25},{10,2},{18... | collective-permute-start | bytes 221192 | tf_op jit(solution)/shard_map/ppermute | solution.py:279
  174.7 3.3 %copy-start.16 = (bf16[3,32,384]{2,1,0:T(8,128)(2,1)}, bf16[3,32,384]{2,1,0:T(8,128)(2,1)S(1)}, u32[]{:S(2)}) copy-start(bf16[3,32,384]{2,1,0:T(8,128)(2,1)S(1)} %collective-permute-done.6.refs_0_) | copy-start | bytes 221188
  178.0 0.6 copy-start.17
  178.7 11.6 %copy-start.10 = (f32[4,32,256]{2,1,0:T(8,128)S(1)}, f32[4,32,256]{2,1,0:T(8,128)}, u32[]{:S(2)}) copy-start(f32[4,32,256]{2,1,0:T(8,128)} %get-tuple-element.18) | copy-start | bytes 393220
  214.9 5.4 %copy-start.1 = (bf16[192,192]{1,0:T(8,128)(2,1)S(1)}, bf16[192,192]{1,0:T(8,128)(2,1)}, u32[]{:S(2)}) copy-start(bf16[192,192]{1,0:T(8,128)(2,1)} %param.15) | copy-start | bytes 221188

commit v2 on v1

--- a/solution.py
+++ b/solution.py
@@ -18,6 +18,15 @@
 F32 = jnp.float32
 
 
+WEIGHTS = ("w_in", "w_a", "w_b", "w_c", "w_out", "coef", "emb", "low")
+OPERANDS = (
+    ("x", "z") + WEIGHTS,
+    ("above", "state", "below", "x", "z") + WEIGHTS,
+    ("above", "state", "below", "z") + WEIGHTS,
+    ("above", "state", "below", "old", "z") + WEIGHTS,
+)
+
+
 def silu(v):
     half = 0.5 * v
     return half + half * jnp.tanh(half)
@@ -29,24 +38,36 @@
     mid_cols, first_cols = out_cols + 2, out_cols + 4
     lanes = -(-out_cols * CH // 128) * 128
     groups_1 = -(-first_cols // 4)
-    if sweep == 0:
-        x_ref, z_ref, coef, emb, w_in, w_a, w_b, w_c, w_out, low = refs[:10]
-        state_out, up_out, down_out = refs[10:13]
-    elif sweep == 1:
-        u_ref, s_ref, d_ref, x_ref, z_ref, coef, emb, w_in, w_a, w_b, w_c, w_out, low = refs[:13]
-        traj_out, state_out, up_out, down_out = refs[13:17]
-    elif sweep == 2:
-        u_ref, s_ref, d_ref, z_ref, coef, emb, w_in, w_a, w_b, w_c, w_out, low = refs[:12]
-        state_out, up_out, down_out = refs[12:15]
-    else:
-        u_ref, s_ref, d_ref, old_ref, z_ref, coef, emb, w_in, w_a, w_b, w_c, w_out, low = refs[:13]
-        traj_out = refs[13]
-    hs, f1, f2 = refs[-3:]
+    names = OPERANDS[sweep]
+    count = len(names)
+    outs = refs[count : -count - 4]
+    held = refs[-count - 4 : -4]
+    hs, f1, f2, sem = refs[-4:]
+    pending = {
+        name: pltpu.make_async_copy(refs[i], held[i], sem.at[i]) for i, name in enumerate(names)
+    }
+    for copy in pending.values():
+        copy.start()
+
+    def fetch(*wanted):
+        for name in wanted:
+            if name in pending:
+                pending.pop(name).wait()
+
+    have = dict(zip(names, held))
+    x_ref, u_ref, s_ref, d_ref = (have.get(n) for n in ("x", "above", "state", "below"))
+    old_ref, z_ref, coef, emb = (have.get(n) for n in ("old", "z", "coef", "emb"))
+    w_in, w_a, w_b, w_c, w_out = (have[n] for n in ("w_in", "w_a", "w_b", "w_c", "w_out"))
+    low = have["low"]
+    outs = list(outs)
+    traj_out = outs.pop(0) if sweep in (1, 3) else None
+    if sweep < 3:
+        state_out, up_out, down_out = outs
     batch = hs.shape[2]
 
+    fetch(*(("x",) if sweep == 0 else ("above", "state", "below")))
     for y in range(ROWS + 6):
         if sweep == 0:
-            row = x_ref[y].astype(BF)
             row = jnp.concatenate([x_ref[y]] * 2, axis=0).astype(BF)
         elif y < 3:
             row = u_ref[y]
@@ -57,20 +78,41 @@
         for g in range(groups_1):
             hs[g, y] = row[:, 64 * g : 64 * g + 128]
 
-    def stage_1(g, _):
-        lhs = jnp.concatenate([hs[g, a : a + ROWS + 4] for a in range(3)], axis=-1)
-        lhs = lhs.reshape((ROWS + 4) * batch, 384)
+    rows_1 = (ROWS + 4) * batch
+
+    def stage_1(gs):
+        lhs = [
+            jnp.concatenate([hs[g, a : a + ROWS + 4] for a in range(3)], axis=-1).reshape(rows_1, 384)
+            for g in gs
+        ]
+        lhs = jnp.concatenate(lhs, axis=0) if len(lhs) > 1 else lhs[0]
         for ph in range(3):
-            acc = jnp.dot(lhs, w_in[ph], preferred_element_type=F32)
-            acc = acc.reshape(ROWS + 4, batch, 256)
-            if batch < SLOTS:
-                acc = jnp.concatenate([acc] * (SLOTS // batch), axis=1)
-            acc = silu(acc + emb[ph][None])
-            at = pl.multiple_of(768 * g + 256 * ph, 256)
-            f1[:, :, pl.ds(at, 256)] = acc.astype(BF)
-        return 0
-
-    lax.fori_loop(0, groups_1, stage_1, 0)
+            total = jnp.dot(lhs, w_in[ph], preferred_element_type=F32)
+            for i, g in enumerate(gs):
+                acc = total[i * rows_1 : (i + 1) * rows_1].reshape(ROWS + 4, batch, 256)
+                if batch < SLOTS:
+                    acc = jnp.concatenate([acc] * (SLOTS // batch), axis=1)
+                acc = silu(acc + emb[sweep // 2, ph][None])
+                f1[:, :, pl.ds(aligned(g, 256 * ph), 256)] = acc.astype(BF)
+
+    def aligned(g, off):
+        at = 768 * g + off
+        return at if isinstance(g, int) else pl.multiple_of(at, 128)
+
+    def over(count, size, stage):
+        def many(i, _):
+            stage([i * size + k for k in range(size)])
+            return 0
+
+        if count // size > 1:
+            lax.fori_loop(0, count // size, many, 0)
+        else:
+            stage(list(range(size)))
+        if count % size:
+            stage(list(range(count - count % size, count)))
+
+    fetch("w_in", "emb")
+    over(groups_1, min(merge[0], groups_1), stage_1)
 
     def clear(ref, ahead, height, top, bottom):
         width = ref.shape[2]
@@ -98,12 +140,12 @@
     mid_rows = ROWS + 2
 
     def window(g, off, length):
-        at = pl.multiple_of(768 * g + off, 128) if not isinstance(g, int) else 768 * g + off
+        at = aligned(g, off)
         part = [f1[a : a + mid_rows, :, pl.ds(at, length)] for a in range(3)]
         return jnp.concatenate(part, axis=-1).reshape(mid_rows * SLOTS, 3 * length)
 
     def put(g, off, acc):
-        at = pl.multiple_of(768 * g + off, 128) if not isinstance(g, int) else 768 * g + off
+        at = aligned(g, off)
         size = acc.shape[-1]
         f2[:, :, pl.ds(at, size)] = silu(acc).astype(BF).reshape(mid_rows, SLOTS, size)
 
@@ -118,14 +160,8 @@
             for i, g in enumerate(gs):
                 put(g, shift, acc[i * rows_2 : (i + 1) * rows_2])
 
-    def many(i, _):
-        stage_2([i * merge + k for k in range(merge)])
-        return 0
-
-    lax.fori_loop(0, groups_2 // merge, many, 0)
-    rest = groups_2 % merge
-    if rest:
-        stage_2([groups_2 - rest + k for k in range(rest)])
+    fetch("w_a", "w_b", "w_c")
+    over(groups_2, min(merge[1], groups_2), stage_2)
     if mid_cols % 4:
         g = groups_2
         acc = jnp.dot(
@@ -136,6 +172,7 @@
         put(g, 256, jnp.dot(window(g, 128, 640), w, preferred_element_type=F32))
     clear(f2, extra + 1, mid_rows, 1, 1)
 
+    fetch(*list(pending))
     full = out_cols // 8
     lhs = [
         jnp.concatenate([f2[a : a + ROWS, :, 1536 * n : 1536 * n + 1920] for a in range(3)], axis=-1)
@@ -156,9 +193,7 @@
         pieces.append(acc.reshape(ROWS, SLOTS, 128))
     predicted = jnp.concatenate(pieces, axis=-1)
 
-    keep = coef[0][:, 0:1]
-    predict = coef[1][:, 0:1]
-    spread = coef[2][:, 0:1]
+    keep, predict, spread = (coef[sweep // 2, k, :, 0:1] for k in range(3))
     z_at = STEP if sweep in (1, 3) else 0
     where = lax.broadcasted_iota(jnp.int32, (1, lanes), 1)
     low_lane = jnp.where(flags[0] == 1, extra * CH, 0)
@@ -211,56 +246,115 @@
     if sweep < 3:
         shapes.append(jax.ShapeDtypeStruct((ROWS, SLOTS, lanes), F32))
         shapes += [jax.ShapeDtypeStruct((3, SLOTS, lanes), BF)] * 2
+    operands = [args[name] for name in OPERANDS[sweep]]
     vmem = pl.BlockSpec(memory_space=pltpu.VMEM)
-    out = pl.pallas_call(
+    return pl.pallas_call(
         functools.partial(sweep_body, sweep, merge),
         out_shape=tuple(shapes),
-        in_specs=[pl.BlockSpec(memory_space=pltpu.SMEM)] + [vmem] * len(args),
+        in_specs=[pl.BlockSpec(memory_space=pltpu.SMEM)]
+        + [pl.BlockSpec(memory_space=pl.ANY)] * len(operands),
         out_specs=tuple([vmem] * len(shapes)),
-        scratch_shapes=[
+        scratch_shapes=[pltpu.VMEM(o.shape, o.dtype) for o in operands]
+        + [
             pltpu.VMEM((groups_1, ROWS + 6, 16 if sweep == 0 else SLOTS, 128), BF),
             pltpu.VMEM((ROWS + 4, SLOTS, f1_lanes), BF),
             pltpu.VMEM((ROWS + 2, SLOTS, (out_cols + 2) * HID), BF),
+            pltpu.SemaphoreType.DMA((len(operands),)),
         ],
         name=f"sweep{sweep}",
-    )(flags, *args)
-    return out
-
-
-def plan_values(sched, time_weight, hidden):
-    count = sched.shape[0] - 1
-    step = jnp.arange(STEPS)
+    )(flags, *operands)
+
+
+def prepare_body(now_ref, after_ref, in_ref, mid_ref, out_ref, time_ref, w_in, w_a, w_b, w_c, w_out, table, emb):
+    w_in[...] = jnp.zeros_like(w_in)
+    for ref in (w_a, w_b, w_c):
+        ref[...] = jnp.zeros_like(ref)
+    spots = ((w_a, 0, 768, 0), (w_b, 128, 896, 256), (w_c, 384, 768, 512))
+    for a in range(3):
+        for b in range(3):
+            tap = in_ref[a, b]
+            for p in range(4):
+                row = a * 128 + (p + b) * CH
+                for ph in range(3):
+                    lo, hi = max(HID * p, 256 * ph), min(HID * (p + 1), 256 * (ph + 1))
+                    if lo < hi:
+                        w_in[ph, row : row + CH, lo - 256 * ph : hi - 256 * ph] = tap[:, lo - HID * p : hi - HID * p]
+            tap = mid_ref[a, b].astype(F32).T.astype(BF)
+            for p in range(4):
+                row = (p + b) * HID
+                for ref, start, length, lane in spots:
+                    lo, hi = max(HID * p, lane), min(HID * (p + 1), lane + 256)
+                    top, end = max(row, start), min(row + HID, start + length)
+                    if lo < hi and top < end:
+                        ref[a, top - start : end - start, lo - lane : hi - lane] = tap[
+                            top - row : end - row, lo - HID * p : hi - HID * p
+                        ]
+    lane = lax.broadcasted_iota(jnp.int32, (1, 128), 1)
+    spread_out = (lax.broadcasted_iota(jnp.int32, (CH, 128), 1) % CH == lax.broadcasted_iota(jnp.int32, (CH, 128), 0))
+    spread_out = jnp.where(spread_out, 1.0, 0.0).astype(BF)
+    for a in range(3):
+        taps = [jnp.dot(out_ref[a, b], spread_out, preferred_element_type=F32) for b in range(3)]
+        for x in range(10):
+            block = jnp.zeros((HID, 128), F32)
+            for b in range(3):
+                if 0 <= x - b < 8:
+                    at = jnp.where(lane // CH == x - b, 1.0, 0.0)
+                    block = block + taps[b] * at
+            w_out[a, HID * x : HID * (x + 1)] = block.astype(BF)
+
+    now, after = now_ref[...], after_ref[...]
+    step = lax.broadcasted_iota(jnp.int32, (1, 1024), 1)
     betas = 0.0001 + (0.02 - 0.0001) * step.astype(F32) / (STEPS - 1)
-    logs = jnp.log(1.0 - betas)[None]
-    now, after = sched[:count, None], sched[1:, None]
-    log_now = jnp.sum(jnp.where(step[None] <= now, logs, 0.0), axis=1)
-    log_after = jnp.sum(jnp.where(step[None] <= after, logs, 0.0), axis=1)
-    between = (step[None] <= now) & (step[None] > after)
-    retained = jnp.exp(jnp.sum(jnp.where(between, logs, 0.0), axis=1))
+    logs = jnp.where(step < STEPS, jnp.log(1.0 - betas), 0.0)
+    log_now = jnp.sum(jnp.where(step <= now, logs, 0.0), axis=1, keepdims=True)
+    log_after = jnp.sum(jnp.where(step <= after, logs, 0.0), axis=1, keepdims=True)
+    between = jnp.where(step <= now, logs, 0.0) - jnp.where(step <= after, logs, 0.0)
+    retained = jnp.exp(jnp.sum(between, axis=1, keepdims=True))
     bar_now, bar_after = jnp.exp(log_now), jnp.exp(log_after)
     keep = 1.0 / jnp.sqrt(retained) - 1.0
     predict = -(1.0 - retained) / (jnp.sqrt(1.0 - bar_now) * jnp.sqrt(retained))
     spread = jnp.sqrt((1.0 - bar_after) / (1.0 - bar_now) * (1.0 - retained))
-    half = hidden // 2
-    freqs = jnp.exp(-9.210340371976184 * jnp.arange(half).astype(F32) / half)
+    half = HID // 2
+    freqs = jnp.exp(
+        -9.210340371976184 * lax.broadcasted_iota(jnp.int32, (1, half), 1).astype(F32) / half
+    )
     angles = now.astype(F32) * freqs
     features = jnp.concatenate([jnp.sin(angles), jnp.cos(angles)], axis=-1)
-    embedding = jnp.dot(features, time_weight.astype(F32), precision=lax.Precision.HIGHEST)
-    return jnp.stack([keep, predict, spread]), embedding
-
-
-def banded_weights(conv_in, conv_mid, conv_out):
-    w = conv_in.transpose(0, 1, 3, 2)
-    w_in = jnp.stack([jnp.pad(w, ((0, 0), (p, 5 - p), (0, 0), (0, 0))) for p in range(4)], axis=3)
-    w_in = w_in.reshape(3 * 8 * CH, 3, 256).transpose(1, 0, 2)
-    w = conv_mid.transpose(0, 1, 3, 2)
-    w = jnp.stack([jnp.pad(w, ((0, 0), (p, 3 - p), (0, 0), (0, 0))) for p in range(4)], axis=3)
-    w = w.reshape(3, 6 * HID, 4 * HID)
-    w_a, w_b, w_c = w[:, 0:768, 0:256], w[:, 128:1024, 256:512], w[:, 384:1152, 512:768]
-    w = conv_out.transpose(0, 1, 3, 2)
-    w = jnp.stack([jnp.pad(w, ((0, 0), (p, 7 - p), (0, 0), (0, 0))) for p in range(8)], axis=3)
-    w_out = w.reshape(3, 10 * HID, 8 * CH)
-    return [w_in, w_a, w_b, w_c, w_out]
+    embedding = jnp.dot(
+        features, time_ref[...].astype(F32), preferred_element_type=F32, precision=lax.Precision.HIGHEST
+    )
+    wide = jnp.concatenate([embedding] * 4, axis=-1)
+    for r in range(2):
+        rows = slice(RETIRE * r, RETIRE * r + SLOTS)
+        for k, value in enumerate((keep, predict, spread)):
+            table[r, k] = jnp.broadcast_to(value, (value.shape[0], 128))[rows]
+        for ph in range(3):
+            emb[r, ph] = wide[rows, 256 * ph : 256 * ph + 256]
+
+
+def prepare(sched, conv_in, conv_mid, conv_out, time_weight):
+    now = jnp.pad(sched[:37], (0, 3), constant_values=999)[:, None]
+    after = jnp.pad(sched[1:], (0, 3), constant_values=998)[:, None]
+    shapes = [
+        jax.ShapeDtypeStruct(s, d)
+        for s, d in (
+            ((3, 384, 256), BF),
+            ((3, 768, 256), BF),
+            ((3, 896, 256), BF),
+            ((3, 768, 256), BF),
+            ((3, 1920, 128), BF),
+            ((2, 3, SLOTS, 128), F32),
+            ((2, 3, SLOTS, 256), F32),
+        )
+    ]
+    vmem = pl.BlockSpec(memory_space=pltpu.VMEM)
+    return pl.pallas_call(
+        prepare_body,
+        out_shape=tuple(shapes),
+        in_specs=[vmem] * 6,
+        out_specs=tuple([vmem] * len(shapes)),
+        name="prepare",
+    )(now, after, conv_in.transpose(0, 1, 3, 2), conv_mid, conv_out.transpose(0, 1, 3, 2), time_weight)
 
 
 def shards(x_start, noise, fresh, sched, conv_in, conv_mid, conv_out, time_weight):
@@ -303,14 +397,7 @@
     z9 = jnp.pad(got[:, :, 0:544].astype(F32), ((0, 0), (0, 0), (0, 96)))
     z9 = z9 + jnp.pad(got[:, :, 544:800].astype(F32), ((0, 0), (0, 0), (144, 240)))
 
-    weights = banded_weights(conv_in, conv_mid, conv_out)
-    values, embedding = plan_values(sched, time_weight, HID)
-
-    def coefs(r):
-        mine = values[:, RETIRE * r : RETIRE * r + SLOTS]
-        table = jnp.broadcast_to(mine[:, :, None], (3, SLOTS, 128))
-        emb = jnp.tile(embedding[RETIRE * r : RETIRE * r + SLOTS], (1, 4))
-        return table, emb.reshape(SLOTS, 3, 256).transpose(1, 0, 2)
+    *weights, table, emb = prepare(sched, conv_in, conv_mid, conv_out, time_weight)
 
     i, j = jnp.arange(SLOTS)[None], jnp.arange(SLOTS)[:, None]
     low = (i < j).astype(F32)
@@ -326,40 +413,36 @@
         ]
     ).astype(jnp.int32)
 
-    f = fresh[:, 0].transpose(2, 0, 3, 1)
-    f = jnp.pad(f, ((0, 0), (0, 0), (3, 5), (0, 0))).reshape(16, RETIRE, 136 * CH)
-    f = lax.dynamic_slice(f, (quarter * ROWS, 0, column * 256), (ROWS, RETIRE, 384))
-    lane = jnp.arange(384)
-    f = jnp.where(lane < 352, f, 0.0)
+    f = jnp.pad(fresh[:, 0], ((0, 0), (0, 0), (0, 0), (3, 5)))
+    f = lax.dynamic_slice(f, (0, 0, quarter * ROWS, column * COLS), (RETIRE, CH, ROWS, 24))
+    f = f.transpose(2, 0, 3, 1).reshape(ROWS, RETIRE, 384)
+    f = jnp.where(jnp.arange(384) < 352, f, 0.0)
     z3 = jnp.concatenate([z9[:, RETIRE:, 96:480], f], axis=1)
 
     x = jnp.concatenate([above.astype(F32), latent, below.astype(F32)], axis=1)
-    x = jnp.pad(x.transpose(1, 2, 0), ((0, 0), (12, 20), (0, 0))).reshape(22, 160 * CH)
-    x = lax.dynamic_slice(x, (quarter * ROWS, column * 256), (ROWS + 6, 768))
-    x = jnp.broadcast_to(x[:, None], (ROWS + 6, 8, 768))
-
-    table, emb = coefs(0)
-    s1, to_upper, to_lower = sweep_call(0, MERGE, flags, [x, z9, table, emb, *weights, low])
+    x = jnp.pad(x, ((0, 0), (0, 0), (12, 20)))
+    x = lax.dynamic_slice(x, (0, quarter * ROWS, column * COLS), (CH, ROWS + 6, 48))
+    x = x.transpose(1, 2, 0).reshape(ROWS + 6, 1, 768)
+    x = jnp.broadcast_to(x, (ROWS + 6, 8, 768))
+
+    args = dict(zip(("w_in", "w_a", "w_b", "w_c", "w_out"), weights), coef=table, emb=emb, x=x, z=z9, low=low)
+    s1, to_upper, to_lower = sweep_call(0, MERGE[0], flags, args)
     above, below = rim(to_upper, to_lower)
-    first_out, s2, to_upper, to_lower = sweep_call(
-        1, MERGE, flags, [above, s1, below, x, z9, table, emb, *weights, low_2]
-    )
+    args.update(above=above, state=s1, below=below, low=low_2)
+    first_out, s2, to_upper, to_lower = sweep_call(1, MERGE[1], flags, args)
     above, below = rim(to_upper, to_lower)
-    table, emb = coefs(1)
-    s3, to_upper, to_lower = sweep_call(
-        2, MERGE, flags, [above, s2, below, z3, table, emb, *weights, low]
-    )
+    args.update(above=above, state=s2, below=below, low=low, z=z3)
+    s3, to_upper, to_lower = sweep_call(2, MERGE[2], flags, args)
     above, below = rim(to_upper, to_lower)
-    (second_out,) = sweep_call(
-        3, MERGE, flags, [above, s3, below, s2, z3, table, emb, *weights, low]
-    )
+    args.update(above=above, state=s3, below=below, old=s2)
+    (second_out,) = sweep_call(3, MERGE[3], flags, args)
     out = jnp.stack([first_out, second_out]).transpose(2, 0, 1, 3).reshape(SLOTS, 16, 128)
     out = lax.all_to_all(out, "tm", 0, 0, tiled=True)
     out = out.reshape(column_parts, row_parts, 2, ROWS, COLS, CH).transpose(2, 5, 1, 3, 0, 4)
     return out.reshape(2, 1, 1, CH, 16, 128)
 
 
-MERGE = 2
+MERGE = ((2, 4), (2, 4), (2, 4), (1, 3))
 
 
 def solution(mesh):

time: 225 us -> 159 us (0.71); the launches traced: 221 us -> 158 us
  local copies, waits for them, and re-layouts: 77.3 us -> 15.1 us
  other arithmetic: 11.6 us -> 6.11 us
  Pallas kernels: 63 us -> 68 us
    reshape x7 -> x2, local copies, waits for them, and re-layouts: 26.4 us -> 0.27 us  [shards(): f = f.transpose(2, 0, 3, 1).reshape(ROWS, RETIRE, 384)]
    another operation x13 -> x1, local copies, waits for them, and re-layouts: 20.4 us -> 0.01 us  [the longest x2 14.8 us: banded_weights(): jnp.stack([jnp.pad(w, ((0, 0), (p, 3 - p), (0, 0), (0, 0))) for p in rang...]
    slice x5 -> x2, local copies, waits for them, and re-layouts: 5.91 us -> 0.09 us  [the longest x1 0.07 us: prepare(): after = jnp.pad(sched[1:], (0, 3), constant_values=998)[:, None]]
    pad x2 -> x0, local copies, waits for them, and re-layouts: 5.8 us -> none  [the longest x1 5.56 us: shards(): jnp.pad(f, ((0, 0), (0, 0), (3, 5), (0, 0))).reshape(16, RETIRE, 136 * CH)]
    pallas_call x0 -> x1, Pallas kernels: none -> 5.62 us  [prepare(): pl.pallas_call(prepare_body, out_shape=tuple(shapes), in_specs=[vmem] * 6...]
    another operation x4 -> x1, other arithmetic: 5.11 us -> 0.01 us  [the longest x1 3.96 us: banded_weights(): jnp.stack([jnp.pad(w, ((0, 0), (p, 3 - p), (0, 0), (0, 0))) for p in rang...]
    unnamed x50 -> x30, local copies, waits for them, and re-layouts: 6.69 us -> 3.22 us
  transfers between devices with their start and end apart: 9 -> 9, of which waited for: 4 -> 5; matrix products, arithmetic and copies ran while one was open for 34% -> 4% of each run, Pallas kernels for 0% -> 4%
where the time goes in v2:
time: 159 us; the launch traced here: 158 us
  Pallas kernels  68 us (43%)
  starting transfers between devices  38.5 us (24%)
  blocking collectives  22.7 us (14%)
  local copies, waits for them, and re-layouts  15.1 us (9%)
  waiting for transfers between devices  7.47 us (5%)
  other arithmetic  6.11 us (4%)
    pallas_call x4, Pallas kernels, sweep_call(): pl.pallas_call(functools.partial(sweep_body, sweep, merge), out_shape=tup...  62.4 us
    all_to_all x1, blocking collectives, shards(): out = lax.all_to_all(out, 'tm', 0, 0, tiled=True)  22.7 us
    all_to_all x1, starting transfers between devices, shards(): got = lax.all_to_all(sent, 'tm', 0, 0, tiled=True)  12 us
    ppermute x3, starting transfers between devices, rim(): above = lax.ppermute(for_lower, ('tm', 'rows'), down)  10.6 us
    ppermute x3, starting transfers between devices, rim(): below = lax.ppermute(for_upper, ('tm', 'rows'), up)  9.95 us
    ppermute x3, waiting for transfers between devices, rim(): below = lax.ppermute(for_upper, ('tm', 'rows'), up)  6.71 us
    pallas_call x1, Pallas kernels, prepare(): pl.pallas_call(prepare_body, out_shape=tuple(shapes), in_specs=[vmem] * 6...  5.62 us
    ppermute x1, starting transfers between devices, shards(): above = lax.ppermute(latent[:, 13:16].astype(BF), 'rows', strip_down)  4.05 us
  transfers between devices with their start and end apart: 9, of which 5 were waited for; matrix products, arithmetic and copies ran while one was open for 4% of the time, Pallas kernels for 4%

profile of v2, /device:TPU:1, one launch (start us, length us, event | category | flops | bytes accessed | tf_op | source)
XLA Modules:
  0.0 158.4 jit_solution(11226458110933197154)
XLA Ops:
  0.0 0.9 reduce-precision_convert_fusion
  0.9 0.3 copy.33
  1.2 0.5 reshape.40
  1.7 0.1 fusion.22
  1.8 0.3 copy.61
  2.1 0.2 pad.34.clone
  2.3 0.4 reshape.39
  2.8 0.1 pad.71.clone
  2.9 0.1 fusion.11
  3.0 0.1 fusion.12
  3.1 0.1 fusion.13
  3.1 0.1 fusion.14
  3.2 0.1 fusion.15
  3.3 0.1 fusion.16
  3.4 0.1 fusion.17
  3.5 0.1 fusion.18
  3.5 0.8 reshape.41
  4.4 12.0 %all-to-all-start = ((bf16[32,32,128]{2,1,0:T(8,128)(2,1)}), bf16[32,32,128]{2,1,0:T(8,128)(2,1)S(1)}, u32[]{:S(2)}, u32[]{:S(2)}) async-start(bf16[32,32,128]{2,1,0:T(8,128)(2,1)} %reshape.41), calls=%async_computation | async-start | bytes 524288 | tf_op jit(solution)/shard_map/all_to_all | solution.py:395
  16.4 4.0 %collective-permute-start = (bf16[16,3,128]{2,1,0:T(4,128)(2,1)S(1)}, bf16[16,3,128]{2,1,0:T(4,128)(2,1)S(1)}, u32[]{:S(2)}, u32[]{:S(2)}) collective-permute-start(bf16[16,3,128]{2,1,0:T(4,128)(2,1)S(1)} %get-tuple-element.58), channel_id=1, source_target_pairs={{0,1},{1,2},{2,3},{3,4},{4,5},{5,6},{6,7},{8,9},{9,10},{10,11},{11... | collective-permute-start | bytes 36872 | tf_op jit(solution)/shard_map/ppermute | solution.py:380
  20.5 1.9 %collective-permute-start.1 = (bf16[16,3,128]{2,1,0:T(4,128)(2,1)S(1)}, bf16[16,3,128]{2,1,0:T(4,128)(2,1)S(1)}, u32[]{:S(2)}, u32[]{:S(2)}) collective-permute-start(bf16[16,3,128]{2,1,0:T(4,128)(2,1)S(1)} %get-tuple-element.57), channel_id=1, source_target_pairs={{1,0},{2,1},{3,2},{4,3},{5,4},{6,5},{7,6},{9,8},{10,9},{11,10},{12... | collective-permute-start | bytes 36872 | tf_op jit(solution)/shard_map/ppermute | solution.py:381
  22.4 0.6 fusion.19.refs_9_.refs_11_.refs_12_
  23.1 0.2 fusion
  23.3 0.1 copy.51
  23.4 0.1 reshape.47
  23.6 0.6 add_convert_fusion.flags
  24.2 0.7 copy.44.now_ref
  24.9 0.7 copy.45.after_ref
  25.6 1.0 copy.43
  26.5 5.6 %prepare.1 = (bf16[3,384,256]{2,1,0:T(8,128)(2,1)}, bf16[3,768,256]{2,1,0:T(8,128)(2,1)}, bf16[3,896,256]{2,1,0:T(8,128)(2,1)}, bf16[3,768,256]{2,1,0:T(8,128)(2...) custom-call(s32[40,1]{1,0:T(8,128)} %copy.44.now_ref, ...), custom_call_target="tpu_custom_call" | custom-call | tf_op jit(solution)/shard_map/prepare/pallas_call | solution.py:351
  32.2 0.2 fusion.5
  32.4 0.1 copy.31
  32.6 0.1 broadcast_in_dim.23
  32.8 0.1 copy.71
  32.9 0.1 slice.114
  33.0 0.8 convert_add_fusion.refs_1_.refs_4_
  33.8 0.7 broadcast_in_dim.24.refs_0_.refs_3_
  34.5 18.9 %sweep0.1 = (f32[4,32,640]{2,1,0:T(8,128)}, bf16[3,32,640]{2,1,0:T(8,128)(2,1)}, bf16[3,32,640]{2,1,0:T(8,128)(2,1)}) custom-call(s32[4]{0:T(128)} %add_convert_fusion.flags, f32[10,8,768]{2,1,0:T(8,128)} %broadcast_in_dim.24.refs_0_.refs_3_, f32[4,32,640]{2,1,0:T(8,128)} %convert_add_fusion.refs_1_.refs_4_, ...), custom_call_target="tpu_custom_call" | custom-call | tf_op jit(solution)/shard_map/sweep0/pallas_call | solution.py:251
  53.5 3.4 %collective-permute-start.2 = (bf16[3,32,640]{2,1,0:T(8,128)(2,1)}, bf16[3,32,640]{2,1,0:T(8,128)(2,1)S(1)}, u32[]{:S(2)}, u32[]{:S(2)}) collective-permute-start(bf16[3,32,640]{2,1,0:T(8,128)(2,1)} %get-tuple-element.29), channel_id=1, source_target_pairs={{0,8},{8,16},{16,24},{24,1},{1,9},{9,17},{17,25},{25,2},{2,10},{10... | collective-permute-start | bytes 368648 | tf_op jit(solution)/shard_map/ppermute | solution.py:374
  56.9 3.4 %collective-permute-start.3 = (bf16[3,32,640]{2,1,0:T(8,128)(2,1)}, bf16[3,32,640]{2,1,0:T(8,128)(2,1)S(1)}, u32[]{:S(2)}, u32[]{:S(2)}) collective-permute-start(bf16[3,32,640]{2,1,0:T(8,128)(2,1)} %get-tuple-element.31), channel_id=1, source_target_pairs={{8,0},{16,8},{24,16},{1,24},{9,1},{17,9},{25,17},{2,25},{10,2},{18... | collective-permute-start | bytes 368648 | tf_op jit(solution)/shard_map/ppermute | solution.py:373
  60.3 0.6 pad_maximum_fusion.1.refs_12_
  61.0 0.1 slice.115
  61.1 0.4 collective-permute-done.2.refs_0_
  61.5 1.2 collective-permute-done.3.refs_2_
  62.7 0.6 copy-done.6
  63.4 17.6 %sweep1.1 = (f32[4,32,256]{2,1,0:T(8,128)}, f32[4,32,512]{2,1,0:T(8,128)}, bf16[3,32,512]{2,1,0:T(8,128)(2,1)}, bf16[3,32,512]{2,1,0:T(8,128)(2,1)}) custom-call(s32[4]{0:T(128)} %add_convert_fusion.flags, bf16[3,32,640]{2,1,0:T(8,128)(2,1)} %copy-done.5, f32[4,32,640]{2,1,0:T(8,128)} %get-tuple-element.30.refs_1_, bf16[3,32,640]{2,1,0:T(8,128)(2,1)} %copy-done.6, ...), custom_call_target="tpu_custom_call" | custom-call | tf_op jit(solution)/shard_map/sweep1/pallas_call | solution.py:251
  81.0 3.1 %collective-permute-start.4 = (bf16[3,32,512]{2,1,0:T(8,128)(2,1)}, bf16[3,32,512]{2,1,0:T(8,128)(2,1)S(1)}, u32[]{:S(2)}, u32[]{:S(2)}) collective-permute-start(bf16[3,32,512]{2,1,0:T(8,128)(2,1)} %get-tuple-element.33), channel_id=1, source_target_pairs={{0,8},{8,16},{16,24},{24,1},{1,9},{9,17},{17,25},{25,2},{2,10},{10... | collective-permute-start | bytes 294920 | tf_op jit(solution)/shard_map/ppermute | solution.py:374
  84.1 4.0 %collective-permute-start.5 = (bf16[3,32,512]{2,1,0:T(8,128)(2,1)}, bf16[3,32,512]{2,1,0:T(8,128)(2,1)S(1)}, u32[]{:S(2)}, u32[]{:S(2)}) collective-permute-start(bf16[3,32,512]{2,1,0:T(8,128)(2,1)} %get-tuple-element.35), channel_id=1, source_target_pairs={{8,0},{16,8},{24,16},{1,24},{9,1},{17,9},{25,17},{2,25},{10,2},{18... | collective-permute-start | bytes 294920 | tf_op jit(solution)/shard_map/ppermute | solution.py:373
  88.1 0.7 pad_maximum_fusion.refs_3_.refs_4_
  88.8 2.2 %collective-permute-done.5.refs_2_ = bf16[3,32,512]{2,1,0:T(8,128)(2,1)S(1)} collective-permute-done((bf16[3,32,512]{2,1,0:T(8,128)(2,1)}, bf16[3,32,512]{2,1,0:T(8,128)(2,1)S(1)}, u32[]{:S(2)}, u32[]{:S(2)}) %collective-permute-start.5) | collective-permute-done | bytes 98336 | tf_op jit(solution)/shard_map/ppermute | solution.py:373
  91.0 0.6 copy-done.8
  91.6 14.0 %sweep2.1 = (f32[4,32,384]{2,1,0:T(8,128)}, bf16[3,32,384]{2,1,0:T(8,128)(2,1)}, bf16[3,32,384]{2,1,0:T(8,128)(2,1)}) custom-call(s32[4]{0:T(128)} %add_convert_fusion.flags, bf16[3,32,512]{2,1,0:T(8,128)(2,1)} %copy-done.7, f32[4,32,512]{2,1,0:T(8,128)} %get-tuple-element.34.refs_1_.refs_3_, bf16[3,32,512]{2,1,0:T(8,128)(2,1)} %copy-done.8, ...), custom_call_target="tpu_custom_call" | custom-call | tf_op jit(solution)/shard_map/sweep2/pallas_call | solution.py:251
  105.6 4.1 %collective-permute-start.6 = (bf16[3,32,384]{2,1,0:T(8,128)(2,1)}, bf16[3,32,384]{2,1,0:T(8,128)(2,1)S(1)}, u32[]{:S(2)}, u32[]{:S(2)}) collective-permute-start(bf16[3,32,384]{2,1,0:T(8,128)(2,1)} %get-tuple-element.36), channel_id=1, source_target_pairs={{0,8},{8,16},{16,24},{24,1},{1,9},{9,17},{17,25},{25,2},{2,10},{10... | collective-permute-start | bytes 221192 | tf_op jit(solution)/shard_map/ppermute | solution.py:374
  109.8 2.6 %collective-permute-start.7 = (bf16[3,32,384]{2,1,0:T(8,128)(2,1)}, bf16[3,32,384]{2,1,0:T(8,128)(2,1)S(1)}, u32[]{:S(2)}, u32[]{:S(2)}) collective-permute-start(bf16[3,32,384]{2,1,0:T(8,128)(2,1)} %get-tuple-element.38), channel_id=1, source_target_pairs={{8,0},{16,8},{24,16},{1,24},{9,1},{17,9},{25,17},{2,25},{10,2},{18... | collective-permute-start | bytes 221192 | tf_op jit(solution)/shard_map/ppermute | solution.py:373
  112.4 0.3 collective-permute-done.6.refs_0_
  112.7 3.3 %collective-permute-done.7.refs_2_ = bf16[3,32,384]{2,1,0:T(8,128)(2,1)S(1)} collective-permute-done((bf16[3,32,384]{2,1,0:T(8,128)(2,1)}, bf16[3,32,384]{2,1,0:T(8,128)(2,1)S(1)}, u32[]{:S(2)}, u32[]{:S(2)}) %collective-permute-start.7) | collective-permute-done | bytes 73760 | tf_op jit(solution)/shard_map/ppermute | solution.py:373
  116.0 0.6 copy-done.10
  116.7 11.8 %sweep3.1 = f32[4,32,256]{2,1,0:T(8,128)} custom-call(s32[4]{0:T(128)} %add_convert_fusion.flags, bf16[3,32,384]{2,1,0:T(8,128)(2,1)} %copy-done.9, f32[4,32,384]{2,1,0:T(8,128)} %get-tuple-element.37.refs_1_, bf16[3,32,384]{2,1,0:T(8,128)(2,1)} %copy-done.10, f32[4,32,512]{2,1,0:T(8,128)} %get-tuple-element.34.refs_1_.refs_3_, ...), custom_call_target="tpu_custom_call" | custom-call | tf_op jit(solution)/shard_map/sweep3/pallas_call | solution.py:251
  128.5 0.9 maximum_bitcast_fusion
  129.4 0.2 copy.48
  129.6 0.1 reshape.44
  129.7 22.7 %all_to_all.10 = f32[32,16,128]{2,1,0:T(8,128)S(1)} all-to-all(f32[32,16,128]{2,1,0:T(8,128)S(1)} %reshape.44), channel_id=1, replica_groups=mesh['tm'=32,'rows'=8] {'tm'}, dimensions={0} | all-to-all | bytes 524288 | tf_op jit(solution)/shard_map/all_to_all | solution.py:440
  152.4 0.6 reshape.45
  153.0 2.6 %copy.49 = f32[2,16,4,4,8,16]{5,4,3,2,1,0:T(8,128)} copy(f32[2,16,4,4,8,16]{1,5,3,0,2,4:T(8,128)S(1)} %bitcast.83) | data formatting | bytes 524288 | tf_op jit(solution)/shard_map/transpose | solution.py:441
  155.6 2.8 %reshape.46 = f32[2,1,1,16,16,128]{5,4,3,0,2,1:T(8,128)} reshape(f32[2,16,4,4,8,16]{5,4,3,2,1,0:T(8,128)} %copy.49) | data formatting | bytes 524288 | tf_op jit(solution)/shard_map/reshape | solution.py:442
  (46 shorter events, 0.4 us)
Async XLA Ops:
  2.3 14.0 %copy-start.2 = (f32[1,16,16,128]{3,2,1,0:T(8,128)S(1)}, f32[1,16,16,128]{3,2,1,0:T(8,128)}, u32[]{:S(2)}) copy-start(f32[1,16,16,128]{3,2,1,0:T(8,128)} %param.8) | copy-start | bytes 393220
  2.7 20.3 %copy-start.12 = (s32[38]{0:T(128)S(1)}, s32[38]{0:T(128)}, u32[]{:S(2)}) copy-start(s32[38]{0:T(128)} %param.11) | copy-start | bytes 460
  2.7 20.4 %copy-start.1 = (f32[5,1,16,16,128]{4,3,2,1,0:T(8,128)S(1)}, f32[5,1,16,16,128]{4,3,2,1,0:T(8,128)}, u32[]{:S(2)}) copy-start(f32[5,1,16,16,128]{4,3,2,1,0:T(8,128)} %param.10) | copy-start | bytes 1966084
  4.4 21.2 %copy-start.11 = (bf16[3,3,16,192]{3,2,1,0:T(8,128)(2,1)S(1)}, bf16[3,3,16,192]{3,2,1,0:T(8,128)(2,1)}, u32[]{:S(2)}) copy-start(bf16[3,3,16,192]{3,2,1,0:T(8,128)(2,1)} %param.14) | copy-start | bytes 165892
  4.4 28.3 %all-to-all-start = ((bf16[32,32,128]{2,1,0:T(8,128)(2,1)}), bf16[32,32,128]{2,1,0:T(8,128)(2,1)S(1)}, u32[]{:S(2)}, u32[]{:S(2)}) async-start(bf16[32,32,128]{2,1,0:T(8,128)(2,1)} %reshape.41), calls=%async_computation | async-start | bytes 524288 | tf_op jit(solution)/shard_map/all_to_all | solution.py:395
  16.4 15.8 %collective-permute-start = (bf16[16,3,128]{2,1,0:T(4,128)(2,1)S(1)}, bf16[16,3,128]{2,1,0:T(4,128)(2,1)S(1)}, u32[]{:S(2)}, u32[]{:S(2)}) collective-permute-start(bf16[16,3,128]{2,1,0:T(4,128)(2,1)S(1)} %get-tuple-element.58), channel_id=1, source_target_pairs={{0,1},{1,2},{2,3},{3,4},{4,5},{5,6},{6,7},{8,9},{9,10},{10,11},{11... | collective-permute-start | bytes 36872 | tf_op jit(solution)/shard_map/ppermute | solution.py:380
  20.5 11.7 %collective-permute-start.1 = (bf16[16,3,128]{2,1,0:T(4,128)(2,1)S(1)}, bf16[16,3,128]{2,1,0:T(4,128)(2,1)S(1)}, u32[]{:S(2)}, u32[]{:S(2)}) collective-permute-start(bf16[16,3,128]{2,1,0:T(4,128)(2,1)S(1)} %get-tuple-element.57), channel_id=1, source_target_pairs={{1,0},{2,1},{3,2},{4,3},{5,4},{6,5},{7,6},{9,8},{10,9},{11,10},{12... | collective-permute-start | bytes 36872 | tf_op jit(solution)/shard_map/ppermute | solution.py:381
  32.2 0.8 copy-start.13
  34.5 25.8 %copy-start.3 = (f32[32,32]{1,0:T(8,128)S(1)}, f32[32,32]{1,0:T(8,128)}, u32[]{:S(2)}) copy-start(f32[32,32]{1,0:T(8,128)} %fusion.19.refs_9_.refs_11_.refs_12_) | copy-start | bytes 12292
  34.5 26.4 %copy-start = (f32[4,32,640]{2,1,0:T(8,128)S(1)}, f32[4,32,640]{2,1,0:T(8,128)}, u32[]{:S(2)}) copy-start(f32[4,32,640]{2,1,0:T(8,128)} %convert_add_fusion.refs_1_.refs_4_) | copy-start | bytes 983044
  53.5 8.1 %collective-permute-start.2 = (bf16[3,32,640]{2,1,0:T(8,128)(2,1)}, bf16[3,32,640]{2,1,0:T(8,128)(2,1)S(1)}, u32[]{:S(2)}, u32[]{:S(2)}) collective-permute-start(bf16[3,32,640]{2,1,0:T(8,128)(2,1)} %get-tuple-element.29), channel_id=1, source_target_pairs={{0,8},{8,16},{16,24},{24,1},{1,9},{9,17},{17,25},{25,2},{2,10},{10... | collective-permute-start | bytes 368648 | tf_op jit(solution)/shard_map/ppermute | solution.py:374
  56.9 5.8 %collective-permute-start.3 = (bf16[3,32,640]{2,1,0:T(8,128)(2,1)}, bf16[3,32,640]{2,1,0:T(8,128)(2,1)S(1)}, u32[]{:S(2)}, u32[]{:S(2)}) collective-permute-start(bf16[3,32,640]{2,1,0:T(8,128)(2,1)} %get-tuple-element.31), channel_id=1, source_target_pairs={{8,0},{16,8},{24,16},{1,24},{9,1},{17,9},{25,17},{2,25},{10,2},{18... | collective-permute-start | bytes 368648 | tf_op jit(solution)/shard_map/ppermute | solution.py:373
  61.5 1.2 copy-start.5
  62.7 0.6 copy-start.6
  81.0 7.8 %collective-permute-start.4 = (bf16[3,32,512]{2,1,0:T(8,128)(2,1)}, bf16[3,32,512]{2,1,0:T(8,128)(2,1)S(1)}, u32[]{:S(2)}, u32[]{:S(2)}) collective-permute-start(bf16[3,32,512]{2,1,0:T(8,128)(2,1)} %get-tuple-element.33), channel_id=1, source_target_pairs={{0,8},{8,16},{16,24},{24,1},{1,9},{9,17},{17,25},{25,2},{2,10},{10... | collective-permute-start | bytes 294920 | tf_op jit(solution)/shard_map/ppermute | solution.py:374
  84.1 6.9 %collective-permute-start.5 = (bf16[3,32,512]{2,1,0:T(8,128)(2,1)}, bf16[3,32,512]{2,1,0:T(8,128)(2,1)S(1)}, u32[]{:S(2)}, u32[]{:S(2)}) collective-permute-start(bf16[3,32,512]{2,1,0:T(8,128)(2,1)} %get-tuple-element.35), channel_id=1, source_target_pairs={{8,0},{16,8},{24,16},{1,24},{9,1},{17,9},{25,17},{2,25},{10,2},{18... | collective-permute-start | bytes 294920 | tf_op jit(solution)/shard_map/ppermute | solution.py:373
  88.8 2.2 %copy-start.7 = (bf16[3,32,512]{2,1,0:T(8,128)(2,1)}, bf16[3,32,512]{2,1,0:T(8,128)(2,1)S(1)}, u32[]{:S(2)}) copy-start(bf16[3,32,512]{2,1,0:T(8,128)(2,1)S(1)} %collective-permute-done.4.refs_0_) | copy-start | bytes 294916
  91.0 0.6 copy-start.8
  105.6 7.1 %collective-permute-start.6 = (bf16[3,32,384]{2,1,0:T(8,128)(2,1)}, bf16[3,32,384]{2,1,0:T(8,128)(2,1)S(1)}, u32[]{:S(2)}, u32[]{:S(2)}) collective-permute-start(bf16[3,32,384]{2,1,0:T(8,128)(2,1)} %get-tuple-element.36), channel_id=1, source_target_pairs={{0,8},{8,16},{16,24},{24,1},{1,9},{9,17},{17,25},{25,2},{2,10},{10... | collective-permute-start | bytes 221192 | tf_op jit(solution)/shard_map/ppermute | solution.py:374
  109.8 6.3 %collective-permute-start.7 = (bf16[3,32,384]{2,1,0:T(8,128)(2,1)}, bf16[3,32,384]{2,1,0:T(8,128)(2,1)S(1)}, u32[]{:S(2)}, u32[]{:S(2)}) collective-permute-start(bf16[3,32,384]{2,1,0:T(8,128)(2,1)} %get-tuple-element.38), channel_id=1, source_target_pairs={{8,0},{16,8},{24,16},{1,24},{9,1},{17,9},{25,17},{2,25},{10,2},{18... | collective-permute-start | bytes 221192 | tf_op jit(solution)/shard_map/ppermute | solution.py:373
  112.7 3.3 %copy-start.9 = (bf16[3,32,384]{2,1,0:T(8,128)(2,1)}, bf16[3,32,384]{2,1,0:T(8,128)(2,1)S(1)}, u32[]{:S(2)}) copy-start(bf16[3,32,384]{2,1,0:T(8,128)(2,1)S(1)} %collective-permute-done.6.refs_0_) | copy-start | bytes 221188
  116.0 0.6 copy-start.10
  116.6 11.8 %copy-start.4 = (f32[4,32,256]{2,1,0:T(8,128)S(1)}, f32[4,32,256]{2,1,0:T(8,128)}, u32[]{:S(2)}) copy-start(f32[4,32,256]{2,1,0:T(8,128)} %get-tuple-element.32) | copy-start | bytes 393220

commit v3 on v2

--- a/solution.py
+++ b/solution.py
@@ -46,8 +46,9 @@
     pending = {
         name: pltpu.make_async_copy(refs[i], held[i], sem.at[i]) for i, name in enumerate(names)
     }
-    for copy in pending.values():
-        copy.start()
+    early = ("x",) if sweep == 0 else ("above", "state", "below")
+    for name in early + ("w_in", "emb"):
+        pending[name].start()
 
     def fetch(*wanted):
         for name in wanted:
@@ -65,7 +66,7 @@
         state_out, up_out, down_out = outs
     batch = hs.shape[2]
 
-    fetch(*(("x",) if sweep == 0 else ("above", "state", "below")))
+    fetch(*early)
     for y in range(ROWS + 6):
         if sweep == 0:
             row = jnp.concatenate([x_ref[y]] * 2, axis=0).astype(BF)
@@ -112,6 +113,9 @@
             stage(list(range(count - count % size, count)))
 
     fetch("w_in", "emb")
+    for name in ("w_a", "w_b", "w_c", "w_out", "z", "x", "old", "coef", "low"):
+        if name in pending:
+            pending[name].start()
     over(groups_1, min(merge[0], groups_1), stage_1)
 
     def clear(ref, ahead, height, top, bottom):
@@ -265,7 +269,7 @@
     )(flags, *operands)
 
 
-def prepare_body(now_ref, after_ref, in_ref, mid_ref, out_ref, time_ref, w_in, w_a, w_b, w_c, w_out, table, emb):
+def prepare_body(plan_ref, in_ref, mid_ref, out_ref, time_ref, w_in, w_a, w_b, w_c, w_out, table, emb):
     w_in[...] = jnp.zeros_like(w_in)
     for ref in (w_a, w_b, w_c):
         ref[...] = jnp.zeros_like(ref)
@@ -302,7 +306,7 @@
                     block = block + taps[b] * at
             w_out[a, HID * x : HID * (x + 1)] = block.astype(BF)
 
-    now, after = now_ref[...], after_ref[...]
+    now, after = plan_ref[:, 0:1], plan_ref[:, 1:2]
     step = lax.broadcasted_iota(jnp.int32, (1, 1024), 1)
     betas = 0.0001 + (0.02 - 0.0001) * step.astype(F32) / (STEPS - 1)
     logs = jnp.where(step < STEPS, jnp.log(1.0 - betas), 0.0)
@@ -333,8 +337,7 @@
 
 
 def prepare(sched, conv_in, conv_mid, conv_out, time_weight):
-    now = jnp.pad(sched[:37], (0, 3), constant_values=999)[:, None]
-    after = jnp.pad(sched[1:], (0, 3), constant_values=998)[:, None]
+    plan = jnp.pad(jnp.stack([sched[:37], sched[1:]], axis=1), ((0, 3), (0, 0)), mode="edge")
     shapes = [
         jax.ShapeDtypeStruct(s, d)
         for s, d in (
@@ -351,10 +354,10 @@
     return pl.pallas_call(
         prepare_body,
         out_shape=tuple(shapes),
-        in_specs=[vmem] * 6,
+        in_specs=[vmem] * 5,
         out_specs=tuple([vmem] * len(shapes)),
         name="prepare",
-    )(now, after, conv_in.transpose(0, 1, 3, 2), conv_mid, conv_out.transpose(0, 1, 3, 2), time_weight)
+    )(plan, conv_in.transpose(0, 1, 3, 2), conv_mid, conv_out.transpose(0, 1, 3, 2), time_weight)
 
 
 def shards(x_start, noise, fresh, sched, conv_in, conv_mid, conv_out, time_weight):
@@ -442,7 +445,7 @@
     return out.reshape(2, 1, 1, CH, 16, 128)
 
 
-MERGE = ((2, 4), (2, 4), (2, 4), (1, 3))
+MERGE = ((2, 4), (1, 3), (2, 4), (1, 3))
 
 
 def solution(mesh):

time: 159 us -> 152 us (0.956)
  Pallas kernels: 68 us -> 61.5 us
    pallas_call x4, Pallas kernels: 62.4 us -> 55.9 us  [sweep_call(): pl.pallas_call(functools.partial(sweep_body, sweep, merge), out_shape=tup...]
where the time goes in v3:
time: 152 us
  Pallas kernels  61.5 us (40%)
  starting transfers between devices  38.6 us (25%)
  blocking collectives  22.7 us (15%)
  local copies, waits for them, and re-layouts  14.7 us (10%)
  waiting for transfers between devices  7.46 us (5%)
  other arithmetic  6.21 us (4%)
    pallas_call x4, Pallas kernels, sweep_call(): pl.pallas_call(functools.partial(sweep_body, sweep, merge), out_shape=tup...  55.9 us
    all_to_all x1, blocking collectives, shards(): out = lax.all_to_all(out, 'tm', 0, 0, tiled=True)  22.7 us
    all_to_all x1, starting transfers between devices, shards(): got = lax.all_to_all(sent, 'tm', 0, 0, tiled=True)  12 us
    ppermute x3, starting transfers between devices, rim(): above = lax.ppermute(for_lower, ('tm', 'rows'), down)  10.7 us
    ppermute x3, starting transfers between devices, rim(): below = lax.ppermute(for_upper, ('tm', 'rows'), up)  9.95 us
    ppermute x3, waiting for transfers between devices, rim(): below = lax.ppermute(for_upper, ('tm', 'rows'), up)  6.68 us
    pallas_call x1, Pallas kernels, prepare(): pl.pallas_call(prepare_body, out_shape=tuple(shapes), in_specs=[vmem] * 5...  5.61 us
    ppermute x1, starting transfers between devices, shards(): above = lax.ppermute(latent[:, 13:16].astype(BF), 'rows', strip_down)  4.05 us
  transfers between devices with their start and end apart: 9, of which 5 were waited for; matrix products, arithmetic and copies ran while one was open for 4% of the time, Pallas kernels for 4%

profile of v3, /device:TPU:1, one launch (start us, length us, event | category | flops | bytes accessed | tf_op | source)
XLA Modules:
  0.0 151.6 jit_solution(14089640121201321280)
XLA Ops:
  0.0 0.9 reduce-precision_convert_fusion
  0.9 0.3 copy.72
  1.2 0.5 reshape.45
  1.7 0.1 fusion.22
  1.8 0.3 copy.99
  2.1 0.2 pad.27.clone
  2.3 0.4 reshape.44
  2.9 0.1 fusion.11
  3.0 0.1 fusion.12
  3.1 0.1 fusion.13
  3.1 0.1 fusion.14
  3.2 0.1 fusion.15
  3.3 0.1 fusion.16
  3.4 0.1 fusion.17
  3.5 0.1 fusion.18
  3.5 0.8 reshape.46
  4.4 12.0 %all-to-all-start = ((bf16[32,32,128]{2,1,0:T(8,128)(2,1)}), bf16[32,32,128]{2,1,0:T(8,128)(2,1)S(1)}, u32[]{:S(2)}, u32[]{:S(2)}) async-start(bf16[32,32,128]{2,1,0:T(8,128)(2,1)} %reshape.46), calls=%async_computation | async-start | bytes 524288 | tf_op jit(solution)/shard_map/all_to_all | solution.py:398
  16.4 4.0 %collective-permute-start = (bf16[16,3,128]{2,1,0:T(4,128)(2,1)S(1)}, bf16[16,3,128]{2,1,0:T(4,128)(2,1)S(1)}, u32[]{:S(2)}, u32[]{:S(2)}) collective-permute-start(bf16[16,3,128]{2,1,0:T(4,128)(2,1)S(1)} %get-tuple-element.58), channel_id=1, source_target_pairs={{0,1},{1,2},{2,3},{3,4},{4,5},{5,6},{6,7},{8,9},{9,10},{10,11},{11... | collective-permute-start | bytes 36872 | tf_op jit(solution)/shard_map/ppermute | solution.py:383
  20.5 1.9 %collective-permute-start.1 = (bf16[16,3,128]{2,1,0:T(4,128)(2,1)S(1)}, bf16[16,3,128]{2,1,0:T(4,128)(2,1)S(1)}, u32[]{:S(2)}, u32[]{:S(2)}) collective-permute-start(bf16[16,3,128]{2,1,0:T(4,128)(2,1)S(1)} %get-tuple-element.57), channel_id=1, source_target_pairs={{1,0},{2,1},{3,2},{4,3},{5,4},{6,5},{7,6},{9,8},{10,9},{11,10},{12... | collective-permute-start | bytes 36872 | tf_op jit(solution)/shard_map/ppermute | solution.py:384
  22.4 0.6 fusion.19.refs_9_.refs_11_.refs_12_
  23.1 0.2 slice_reduce_fusion
  23.4 0.1 pad_add_fusion.1
  23.4 0.2 fusion
  23.6 0.1 copy.89
  23.8 0.1 reshape.53
  23.9 0.6 add_convert_fusion.flags
  24.5 0.7 copy.83.plan_ref
  25.2 1.0 copy.82
  26.2 5.6 %prepare.1 = (bf16[3,384,256]{2,1,0:T(8,128)(2,1)}, bf16[3,768,256]{2,1,0:T(8,128)(2,1)}, bf16[3,896,256]{2,1,0:T(8,128)(2,1)}, bf16[3,768,256]{2,1,0:T(8,128)(2...) custom-call(s32[40,2]{1,0:T(8,128)} %copy.83.plan_ref, ...), custom_call_target="tpu_custom_call" | custom-call | tf_op jit(solution)/shard_map/prepare/pallas_call | solution.py:354
  31.8 0.2 fusion.5
  32.0 0.1 copy.70
  32.2 0.1 broadcast_in_dim.19
  32.4 0.1 copy.109
  32.5 0.1 slice.122
  32.6 0.8 convert_add_fusion.refs_1_.refs_4_
  33.4 0.7 broadcast_in_dim.20.refs_0_.refs_3_
  34.1 17.3 %sweep0.1 = (f32[4,32,640]{2,1,0:T(8,128)}, bf16[3,32,640]{2,1,0:T(8,128)(2,1)}, bf16[3,32,640]{2,1,0:T(8,128)(2,1)}) custom-call(s32[4]{0:T(128)} %add_convert_fusion.flags, f32[10,8,768]{2,1,0:T(8,128)} %broadcast_in_dim.20.refs_0_.refs_3_, f32[4,32,640]{2,1,0:T(8,128)} %convert_add_fusion.refs_1_.refs_4_, ...), custom_call_target="tpu_custom_call" | custom-call | tf_op jit(solution)/shard_map/sweep0/pallas_call | solution.py:255
  51.4 3.4 %collective-permute-start.2 = (bf16[3,32,640]{2,1,0:T(8,128)(2,1)}, bf16[3,32,640]{2,1,0:T(8,128)(2,1)S(1)}, u32[]{:S(2)}, u32[]{:S(2)}) collective-permute-start(bf16[3,32,640]{2,1,0:T(8,128)(2,1)} %get-tuple-element.29), channel_id=1, source_target_pairs={{0,8},{8,16},{16,24},{24,1},{1,9},{9,17},{17,25},{25,2},{2,10},{10... | collective-permute-start | bytes 368648 | tf_op jit(solution)/shard_map/ppermute | solution.py:377
  54.8 3.4 %collective-permute-start.3 = (bf16[3,32,640]{2,1,0:T(8,128)(2,1)}, bf16[3,32,640]{2,1,0:T(8,128)(2,1)S(1)}, u32[]{:S(2)}, u32[]{:S(2)}) collective-permute-start(bf16[3,32,640]{2,1,0:T(8,128)(2,1)} %get-tuple-element.31), channel_id=1, source_target_pairs={{8,0},{16,8},{24,16},{1,24},{9,1},{17,9},{25,17},{2,25},{10,2},{18... | collective-permute-start | bytes 368648 | tf_op jit(solution)/shard_map/ppermute | solution.py:376
  58.3 0.6 pad_maximum_fusion.1.refs_12_
  58.9 0.1 slice.123
  59.0 0.5 collective-permute-done.2.refs_0_
  59.5 1.2 collective-permute-done.3.refs_2_
  60.7 0.6 copy-done.6
  61.3 16.2 %sweep1.1 = (f32[4,32,256]{2,1,0:T(8,128)}, f32[4,32,512]{2,1,0:T(8,128)}, bf16[3,32,512]{2,1,0:T(8,128)(2,1)}, bf16[3,32,512]{2,1,0:T(8,128)(2,1)}) custom-call(s32[4]{0:T(128)} %add_convert_fusion.flags, bf16[3,32,640]{2,1,0:T(8,128)(2,1)} %copy-done.5, f32[4,32,640]{2,1,0:T(8,128)} %get-tuple-element.30.refs_1_, bf16[3,32,640]{2,1,0:T(8,128)(2,1)} %copy-done.6, ...), custom_call_target="tpu_custom_call" | custom-call | tf_op jit(solution)/shard_map/sweep1/pallas_call | solution.py:255
  77.5 3.1 %collective-permute-start.4 = (bf16[3,32,512]{2,1,0:T(8,128)(2,1)}, bf16[3,32,512]{2,1,0:T(8,128)(2,1)S(1)}, u32[]{:S(2)}, u32[]{:S(2)}) collective-permute-start(bf16[3,32,512]{2,1,0:T(8,128)(2,1)} %get-tuple-element.33), channel_id=1, source_target_pairs={{0,8},{8,16},{16,24},{24,1},{1,9},{9,17},{17,25},{25,2},{2,10},{10... | collective-permute-start | bytes 294920 | tf_op jit(solution)/shard_map/ppermute | solution.py:377
  80.6 4.0 %collective-permute-start.5 = (bf16[3,32,512]{2,1,0:T(8,128)(2,1)}, bf16[3,32,512]{2,1,0:T(8,128)(2,1)S(1)}, u32[]{:S(2)}, u32[]{:S(2)}) collective-permute-start(bf16[3,32,512]{2,1,0:T(8,128)(2,1)} %get-tuple-element.35), channel_id=1, source_target_pairs={{8,0},{16,8},{24,16},{1,24},{9,1},{17,9},{25,17},{2,25},{10,2},{18... | collective-permute-start | bytes 294920 | tf_op jit(solution)/shard_map/ppermute | solution.py:376
  84.6 0.7 pad_maximum_fusion.refs_3_.refs_4_
  85.3 2.2 %collective-permute-done.5.refs_2_ = bf16[3,32,512]{2,1,0:T(8,128)(2,1)S(1)} collective-permute-done((bf16[3,32,512]{2,1,0:T(8,128)(2,1)}, bf16[3,32,512]{2,1,0:T(8,128)(2,1)S(1)}, u32[]{:S(2)}, u32[]{:S(2)}) %collective-permute-start.5) | collective-permute-done | bytes 98336 | tf_op jit(solution)/shard_map/ppermute | solution.py:376
  87.5 0.6 copy-done.8
  88.1 12.4 %sweep2.1 = (f32[4,32,384]{2,1,0:T(8,128)}, bf16[3,32,384]{2,1,0:T(8,128)(2,1)}, bf16[3,32,384]{2,1,0:T(8,128)(2,1)}) custom-call(s32[4]{0:T(128)} %add_convert_fusion.flags, bf16[3,32,512]{2,1,0:T(8,128)(2,1)} %copy-done.7, f32[4,32,512]{2,1,0:T(8,128)} %get-tuple-element.34.refs_1_.refs_3_, bf16[3,32,512]{2,1,0:T(8,128)(2,1)} %copy-done.8, ...), custom_call_target="tpu_custom_call" | custom-call | tf_op jit(solution)/shard_map/sweep2/pallas_call | solution.py:255
  100.5 4.1 %collective-permute-start.6 = (bf16[3,32,384]{2,1,0:T(8,128)(2,1)}, bf16[3,32,384]{2,1,0:T(8,128)(2,1)S(1)}, u32[]{:S(2)}, u32[]{:S(2)}) collective-permute-start(bf16[3,32,384]{2,1,0:T(8,128)(2,1)} %get-tuple-element.36), channel_id=1, source_target_pairs={{0,8},{8,16},{16,24},{24,1},{1,9},{9,17},{17,25},{25,2},{2,10},{10... | collective-permute-start | bytes 221192 | tf_op jit(solution)/shard_map/ppermute | solution.py:377
  104.7 2.6 %collective-permute-start.7 = (bf16[3,32,384]{2,1,0:T(8,128)(2,1)}, bf16[3,32,384]{2,1,0:T(8,128)(2,1)S(1)}, u32[]{:S(2)}, u32[]{:S(2)}) collective-permute-start(bf16[3,32,384]{2,1,0:T(8,128)(2,1)} %get-tuple-element.38), channel_id=1, source_target_pairs={{8,0},{16,8},{24,16},{1,24},{9,1},{17,9},{25,17},{2,25},{10,2},{18... | collective-permute-start | bytes 221192 | tf_op jit(solution)/shard_map/ppermute | solution.py:376
  107.3 0.3 collective-permute-done.6.refs_0_
  107.6 3.3 %collective-permute-done.7.refs_2_ = bf16[3,32,384]{2,1,0:T(8,128)(2,1)S(1)} collective-permute-done((bf16[3,32,384]{2,1,0:T(8,128)(2,1)}, bf16[3,32,384]{2,1,0:T(8,128)(2,1)S(1)}, u32[]{:S(2)}, u32[]{:S(2)}) %collective-permute-start.7) | collective-permute-done | bytes 73760 | tf_op jit(solution)/shard_map/ppermute | solution.py:376
  110.9 0.6 copy-done.10
  111.6 10.1 %sweep3.1 = f32[4,32,256]{2,1,0:T(8,128)} custom-call(s32[4]{0:T(128)} %add_convert_fusion.flags, bf16[3,32,384]{2,1,0:T(8,128)(2,1)} %copy-done.9, f32[4,32,384]{2,1,0:T(8,128)} %get-tuple-element.37.refs_1_, bf16[3,32,384]{2,1,0:T(8,128)(2,1)} %copy-done.10, f32[4,32,512]{2,1,0:T(8,128)} %get-tuple-element.34.refs_1_.refs_3_, ...), custom_call_target="tpu_custom_call" | custom-call | tf_op jit(solution)/shard_map/sweep3/pallas_call | solution.py:255
  121.7 0.9 maximum_bitcast_fusion
  122.6 0.2 copy.86
  122.8 0.1 reshape.50
  122.9 22.7 %all_to_all.10 = f32[32,16,128]{2,1,0:T(8,128)S(1)} all-to-all(f32[32,16,128]{2,1,0:T(8,128)S(1)} %reshape.50), channel_id=1, replica_groups=mesh['tm'=32,'rows'=8] {'tm'}, dimensions={0} | all-to-all | bytes 524288 | tf_op jit(solution)/shard_map/all_to_all | solution.py:443
  145.6 0.6 reshape.51
  146.2 2.6 %copy.87 = f32[2,16,4,4,8,16]{5,4,3,2,1,0:T(8,128)} copy(f32[2,16,4,4,8,16]{1,5,3,0,2,4:T(8,128)S(1)} %bitcast.83) | data formatting | bytes 524288 | tf_op jit(solution)/shard_map/transpose | solution.py:444
  148.8 2.8 %reshape.52 = f32[2,1,1,16,16,128]{5,4,3,0,2,1:T(8,128)} reshape(f32[2,16,4,4,8,16]{5,4,3,2,1,0:T(8,128)} %copy.87) | data formatting | bytes 524288 | tf_op jit(solution)/shard_map/reshape | solution.py:445
  (48 shorter events, 0.5 us)
Async XLA Ops:
  2.3 14.0 %copy-start.2 = (f32[1,16,16,128]{3,2,1,0:T(8,128)S(1)}, f32[1,16,16,128]{3,2,1,0:T(8,128)}, u32[]{:S(2)}) copy-start(f32[1,16,16,128]{3,2,1,0:T(8,128)} %param.8) | copy-start | bytes 393220
  2.7 20.3 %copy-start.12 = (s32[38]{0:T(128)S(1)}, s32[38]{0:T(128)}, u32[]{:S(2)}) copy-start(s32[38]{0:T(128)} %param.11) | copy-start | bytes 460
  2.7 20.7 %copy-start.1 = (f32[5,1,16,16,128]{4,3,2,1,0:T(8,128)S(1)}, f32[5,1,16,16,128]{4,3,2,1,0:T(8,128)}, u32[]{:S(2)}) copy-start(f32[5,1,16,16,128]{4,3,2,1,0:T(8,128)} %param.10) | copy-start | bytes 1966084
  4.4 20.8 %copy-start.11 = (bf16[3,3,16,192]{3,2,1,0:T(8,128)(2,1)S(1)}, bf16[3,3,16,192]{3,2,1,0:T(8,128)(2,1)}, u32[]{:S(2)}) copy-start(bf16[3,3,16,192]{3,2,1,0:T(8,128)(2,1)} %param.14) | copy-start | bytes 165892
  4.4 28.0 %all-to-all-start = ((bf16[32,32,128]{2,1,0:T(8,128)(2,1)}), bf16[32,32,128]{2,1,0:T(8,128)(2,1)S(1)}, u32[]{:S(2)}, u32[]{:S(2)}) async-start(bf16[32,32,128]{2,1,0:T(8,128)(2,1)} %reshape.46), calls=%async_computation | async-start | bytes 524288 | tf_op jit(solution)/shard_map/all_to_all | solution.py:398
  16.4 15.4 %collective-permute-start = (bf16[16,3,128]{2,1,0:T(4,128)(2,1)S(1)}, bf16[16,3,128]{2,1,0:T(4,128)(2,1)S(1)}, u32[]{:S(2)}, u32[]{:S(2)}) collective-permute-start(bf16[16,3,128]{2,1,0:T(4,128)(2,1)S(1)} %get-tuple-element.58), channel_id=1, source_target_pairs={{0,1},{1,2},{2,3},{3,4},{4,5},{5,6},{6,7},{8,9},{9,10},{10,11},{11... | collective-permute-start | bytes 36872 | tf_op jit(solution)/shard_map/ppermute | solution.py:383
  20.5 11.4 %collective-permute-start.1 = (bf16[16,3,128]{2,1,0:T(4,128)(2,1)S(1)}, bf16[16,3,128]{2,1,0:T(4,128)(2,1)S(1)}, u32[]{:S(2)}, u32[]{:S(2)}) collective-permute-start(bf16[16,3,128]{2,1,0:T(4,128)(2,1)S(1)} %get-tuple-element.57), channel_id=1, source_target_pairs={{1,0},{2,1},{3,2},{4,3},{5,4},{6,5},{7,6},{9,8},{10,9},{11,10},{12... | collective-permute-start | bytes 36872 | tf_op jit(solution)/shard_map/ppermute | solution.py:384
  31.8 0.8 copy-start.13
  34.1 24.1 %copy-start.3 = (f32[32,32]{1,0:T(8,128)S(1)}, f32[32,32]{1,0:T(8,128)}, u32[]{:S(2)}) copy-start(f32[32,32]{1,0:T(8,128)} %fusion.19.refs_9_.refs_11_.refs_12_) | copy-start | bytes 12292
  34.1 24.7 %copy-start = (f32[4,32,640]{2,1,0:T(8,128)S(1)}, f32[4,32,640]{2,1,0:T(8,128)}, u32[]{:S(2)}) copy-start(f32[4,32,640]{2,1,0:T(8,128)} %convert_add_fusion.refs_1_.refs_4_) | copy-start | bytes 983044
  51.4 8.1 %collective-permute-start.2 = (bf16[3,32,640]{2,1,0:T(8,128)(2,1)}, bf16[3,32,640]{2,1,0:T(8,128)(2,1)S(1)}, u32[]{:S(2)}, u32[]{:S(2)}) collective-permute-start(bf16[3,32,640]{2,1,0:T(8,128)(2,1)} %get-tuple-element.29), channel_id=1, source_target_pairs={{0,8},{8,16},{16,24},{24,1},{1,9},{9,17},{17,25},{25,2},{2,10},{10... | collective-permute-start | bytes 368648 | tf_op jit(solution)/shard_map/ppermute | solution.py:377
  54.8 5.8 %collective-permute-start.3 = (bf16[3,32,640]{2,1,0:T(8,128)(2,1)}, bf16[3,32,640]{2,1,0:T(8,128)(2,1)S(1)}, u32[]{:S(2)}, u32[]{:S(2)}) collective-permute-start(bf16[3,32,640]{2,1,0:T(8,128)(2,1)} %get-tuple-element.31), channel_id=1, source_target_pairs={{8,0},{16,8},{24,16},{1,24},{9,1},{17,9},{25,17},{2,25},{10,2},{18... | collective-permute-start | bytes 368648 | tf_op jit(solution)/shard_map/ppermute | solution.py:376
  59.5 1.2 copy-start.5
  60.7 0.6 copy-start.6
  77.5 7.8 %collective-permute-start.4 = (bf16[3,32,512]{2,1,0:T(8,128)(2,1)}, bf16[3,32,512]{2,1,0:T(8,128)(2,1)S(1)}, u32[]{:S(2)}, u32[]{:S(2)}) collective-permute-start(bf16[3,32,512]{2,1,0:T(8,128)(2,1)} %get-tuple-element.33), channel_id=1, source_target_pairs={{0,8},{8,16},{16,24},{24,1},{1,9},{9,17},{17,25},{25,2},{2,10},{10... | collective-permute-start | bytes 294920 | tf_op jit(solution)/shard_map/ppermute | solution.py:377
  80.6 6.9 %collective-permute-start.5 = (bf16[3,32,512]{2,1,0:T(8,128)(2,1)}, bf16[3,32,512]{2,1,0:T(8,128)(2,1)S(1)}, u32[]{:S(2)}, u32[]{:S(2)}) collective-permute-start(bf16[3,32,512]{2,1,0:T(8,128)(2,1)} %get-tuple-element.35), channel_id=1, source_target_pairs={{8,0},{16,8},{24,16},{1,24},{9,1},{17,9},{25,17},{2,25},{10,2},{18... | collective-permute-start | bytes 294920 | tf_op jit(solution)/shard_map/ppermute | solution.py:376
  85.3 2.2 %copy-start.7 = (bf16[3,32,512]{2,1,0:T(8,128)(2,1)}, bf16[3,32,512]{2,1,0:T(8,128)(2,1)S(1)}, u32[]{:S(2)}) copy-start(bf16[3,32,512]{2,1,0:T(8,128)(2,1)S(1)} %collective-permute-done.4.refs_0_) | copy-start | bytes 294916
  87.5 0.6 copy-start.8
  100.5 7.1 %collective-permute-start.6 = (bf16[3,32,384]{2,1,0:T(8,128)(2,1)}, bf16[3,32,384]{2,1,0:T(8,128)(2,1)S(1)}, u32[]{:S(2)}, u32[]{:S(2)}) collective-permute-start(bf16[3,32,384]{2,1,0:T(8,128)(2,1)} %get-tuple-element.36), channel_id=1, source_target_pairs={{0,8},{8,16},{16,24},{24,1},{1,9},{9,17},{17,25},{25,2},{2,10},{10... | collective-permute-start | bytes 221192 | tf_op jit(solution)/shard_map/ppermute | solution.py:377
  104.7 6.3 %collective-permute-start.7 = (bf16[3,32,384]{2,1,0:T(8,128)(2,1)}, bf16[3,32,384]{2,1,0:T(8,128)(2,1)S(1)}, u32[]{:S(2)}, u32[]{:S(2)}) collective-permute-start(bf16[3,32,384]{2,1,0:T(8,128)(2,1)} %get-tuple-element.38), channel_id=1, source_target_pairs={{8,0},{16,8},{24,16},{1,24},{9,1},{17,9},{25,17},{2,25},{10,2},{18... | collective-permute-start | bytes 221192 | tf_op jit(solution)/shard_map/ppermute | solution.py:376
  107.6 3.3 %copy-start.9 = (bf16[3,32,384]{2,1,0:T(8,128)(2,1)}, bf16[3,32,384]{2,1,0:T(8,128)(2,1)S(1)}, u32[]{:S(2)}) copy-start(bf16[3,32,384]{2,1,0:T(8,128)(2,1)S(1)} %collective-permute-done.6.refs_0_) | copy-start | bytes 221188
  110.9 0.6 copy-start.10
  111.6 10.1 %copy-start.4 = (f32[4,32,256]{2,1,0:T(8,128)S(1)}, f32[4,32,256]{2,1,0:T(8,128)}, u32[]{:S(2)}) copy-start(f32[4,32,256]{2,1,0:T(8,128)} %get-tuple-element.32) | copy-start | bytes 393220
